TPU v7x, 32 devices: a whole 2x2x4 slice. The times are simulated.
32 devices in a mesh: groups: 2 (over y), work: 4 (over z), pol: 2 (over x), vis: 2 (over core).
Axes of the slice: x: 2, y: 2, z: 4, core: 2. Of those that a mesh axis runs over, the one named last changes fastest.
Arguments:
- facets: bfloat16 [128, 4, 8, 2048], P(('groups', 'work'), 'pol', 'vis'), parts along dimension 0, may hold values from -6 to 6
- subgrid_offset: int32 [16], P('groups'), parts along dimension 0, may hold values from 0 to 65535
- tile_subgrid: int32 [64], P(('groups', 'work', 'vis')), parts along dimension 0, may hold values from 0 to 1
- tile_count: int32 [64], P(('groups', 'work', 'vis')), parts along dimension 0, may hold values from 1 to 1024, as said below
- vis_coord: float32 [64, 2, 1024], P(('groups', 'work', 'vis')), parts along dimension 0, may hold values from 0 to 1
- stations: int32 [32, 2, 1024], P(('work', 'vis')), may hold values from 0 to 511
- jones: float32 [8, 1024], P(None, 'groups'), parts along dimension 1, may hold values from -4 to 4
- observed: float32 [64, 4, 2, 1024], P(('groups', 'work', 'vis'), 'pol'), parts along dimension 0, may hold values from -6 to 6
Outputs:
- residual_vis: float32 [64, 4, 2, 1024], P(('groups', 'work', 'vis'), 'pol'), parts along dimension 0
- residual_image: float32 [128, 4, 8, 2048], P(('groups', 'work'), 'pol', 'vis'), parts along dimension 0
There are 2 independent parts, one for each index of `groups`. A program takes and returns all parts, laid end to end along the dimension named above; an argument that names none is the same for every part. Nothing has to cross between parts.
Inputs may be any that keep to these rules, and one draw needn't show every extreme that they name: `tile_subgrid`: blocks are laid out worker by worker, 4 * 2 blocks a worker; each names one of its worker's subgrids. `tile_count`: visibility slots at or beyond the count are padding.
All inputs are finite; a program needn't handle non-finite values.
Results may differ from a plain program's by a relative error of at most 0.025.
Values may be sent and summed in bfloat16 or wider, within the bound.
A program may use at most 128 MiB of HBM per device.

v0:
```python
import math

import jax
import jax.numpy as jnp
from jax import lax
from jax.sharding import PartitionSpec as P

FACETS = 64
FS = 1024
SS = 512
ROWS = 8
SG_DEV = 2


TWO_PI = 2.0 * math.pi


def complex_mul(a, b):
    return (a[0] * b[0] - a[1] * b[1], a[0] * b[1] + a[1] * b[0])


def complex_conj(a):
    return (a[0], -a[1])


def complex_add(a, b):
    return (a[0] + b[0], a[1] + b[1])


def jones_matrix(table, pairs, column):
    picked = jnp.take(table, pairs[:, column, :], axis=1)
    return [
        [(picked[0], picked[4]), (picked[1], picked[5])],
        [(picked[2], picked[6]), (picked[3], picked[7])],
    ]


def pol_matrix(visible):
    return [
        [(visible[:, 2 * i + k, 0], visible[:, 2 * i + k, 1]) for k in range(2)] for i in range(2)
    ]


def pack_matrix(matrix):
    return jnp.stack([jnp.stack(matrix[i][k], 1) for i in range(2) for k in range(2)], 1)


def apply_jones(left, right, visible):
    bright = pol_matrix(visible)
    inner = [
        [
            complex_add(
                complex_mul(left[i][0], bright[0][l]), complex_mul(left[i][1], bright[1][l])
            )
            for l in range(2)
        ]
        for i in range(2)
    ]
    outer = [
        [
            complex_add(
                complex_mul(inner[i][0], complex_conj(right[k][0])),
                complex_mul(inner[i][1], complex_conj(right[k][1])),
            )
            for k in range(2)
        ]
        for i in range(2)
    ]
    return pack_matrix(outer)


def adjoint_jones(left, right, visible):
    resid = pol_matrix(visible)
    inner = [
        [
            complex_add(
                complex_mul(complex_conj(left[0][j]), resid[0][k]),
                complex_mul(complex_conj(left[1][j]), resid[1][k]),
            )
            for k in range(2)
        ]
        for j in range(2)
    ]
    outer = [
        [
            complex_add(
                complex_mul(inner[j][0], right[0][l]), complex_mul(inner[j][1], right[1][l])
            )
            for l in range(2)
        ]
        for j in range(2)
    ]
    return pack_matrix(outer)


def transform_tables():
    image_len = FACETS * FS
    xcells = jnp.arange(FS, dtype=jnp.int32)
    ucells = jnp.arange(SS, dtype=jnp.int32)
    turn = -TWO_PI * (xcells[:, None] * ucells[None, :] % image_len).astype(jnp.float32) / image_len
    cosine = jnp.cos(turn)
    sine_table = jnp.sin(turn)
    forward = jnp.concatenate(
        [jnp.concatenate([cosine, sine_table], 1), jnp.concatenate([-sine_table, cosine], 1)], 0
    )
    backward = jnp.concatenate(
        [
            jnp.concatenate([cosine.T, -sine_table.T], 1),
            jnp.concatenate([sine_table.T, cosine.T], 1),
        ],
        0,
    )
    return (forward.astype(jnp.bfloat16), backward.astype(jnp.bfloat16))


def to_subgrids(facet_blk, facet_start, offsets, forward):
    facet_count = facet_blk.shape[0]
    facet_len = facet_blk.shape[-1] // 2
    subgrid_len = forward.shape[1] // 2
    image_len = FACETS * FS
    number = offsets.shape[0]
    xcells = jnp.arange(facet_len, dtype=jnp.int32)
    turn = (
        -TWO_PI * (xcells[None, :] * offsets[:, None] % image_len).astype(jnp.float32) / image_len
    )
    cosine = jnp.cos(turn)[:, None, None, None, :]
    sine_table = jnp.sin(turn)[:, None, None, None, :]
    real_in = facet_blk[..., :facet_len].astype(jnp.float32)[None]
    imag_in = facet_blk[..., facet_len:].astype(jnp.float32)[None]
    shifted = jnp.concatenate(
        [real_in * cosine - imag_in * sine_table, real_in * sine_table + imag_in * cosine], -1
    ).astype(jnp.bfloat16)
    spectra = jnp.dot(
        shifted.reshape(-1, 2 * facet_len), forward, preferred_element_type=jnp.float32
    )
    spectra = spectra.reshape(
        number, facet_count, facet_blk.shape[1], facet_blk.shape[2], 2 * subgrid_len
    )
    facet_ids = facet_start + jnp.arange(facet_count, dtype=jnp.int32)
    ucells = jnp.arange(subgrid_len, dtype=jnp.int32)
    wraps = facet_ids[None, :, None] * (offsets[:, None, None] + ucells[None, None, :]) % FACETS
    turn_out = -TWO_PI * wraps.astype(jnp.float32) / FACETS
    cosine_out = jnp.cos(turn_out)[:, :, None, None, :]
    sine_out = jnp.sin(turn_out)[:, :, None, None, :]
    real_spec = spectra[..., :subgrid_len]
    imag_spec = spectra[..., subgrid_len:]
    real_sum = jnp.sum(real_spec * cosine_out - imag_spec * sine_out, axis=1)
    imag_sum = jnp.sum(real_spec * sine_out + imag_spec * cosine_out, axis=1)
    return jnp.concatenate([real_sum, imag_sum], -1) / math.sqrt(image_len)


def to_facets(grid_blk, offsets, facet_start, facet_count, backward):
    number = grid_blk.shape[0]
    subgrid_len = grid_blk.shape[-1] // 2
    facet_len = backward.shape[1] // 2
    image_len = FACETS * FS
    facet_ids = facet_start + jnp.arange(facet_count, dtype=jnp.int32)
    ucells = jnp.arange(subgrid_len, dtype=jnp.int32)
    wraps = facet_ids[None, :, None] * (offsets[:, None, None] + ucells[None, None, :]) % FACETS
    turn_in = TWO_PI * wraps.astype(jnp.float32) / FACETS
    cosine_in = jnp.cos(turn_in)[:, :, None, None, :]
    sine_in = jnp.sin(turn_in)[:, :, None, None, :]
    real_in = grid_blk[..., :subgrid_len].astype(jnp.float32)[:, None]
    imag_in = grid_blk[..., subgrid_len:].astype(jnp.float32)[:, None]
    rotated = jnp.concatenate(
        [real_in * cosine_in - imag_in * sine_in, real_in * sine_in + imag_in * cosine_in], -1
    ).astype(jnp.bfloat16)
    images = jnp.dot(
        rotated.reshape(-1, 2 * subgrid_len), backward, preferred_element_type=jnp.float32
    )
    images = images.reshape(
        number, facet_count, grid_blk.shape[1], grid_blk.shape[2], 2 * facet_len
    )
    xcells = jnp.arange(facet_len, dtype=jnp.int32)
    turn_x = (
        TWO_PI * (xcells[None, :] * offsets[:, None] % image_len).astype(jnp.float32) / image_len
    )
    cosine_x = jnp.cos(turn_x)[:, None, None, None, :]
    sine_x = jnp.sin(turn_x)[:, None, None, None, :]
    real_img = images[..., :facet_len]
    imag_img = images[..., facet_len:]
    real_sum = jnp.sum(real_img * cosine_x - imag_img * sine_x, axis=0)
    imag_sum = jnp.sum(real_img * sine_x + imag_img * cosine_x, axis=0)
    return jnp.concatenate([real_sum, imag_sum], -1) / math.sqrt(image_len)


def wave_table(coord):
    columns = jnp.arange(SS, dtype=jnp.int32).astype(jnp.float32)
    turn = TWO_PI * coord[:, 1, :, None] * columns
    return jnp.concatenate([jnp.cos(turn), jnp.sin(turn)], -1).astype(jnp.bfloat16)


def row_phase(coord):
    lines = jnp.arange(ROWS, dtype=jnp.int32).astype(jnp.float32)
    turn = TWO_PI * coord[:, 0, :, None] * lines
    return (jnp.cos(turn), jnp.sin(turn))


def degrid(subs, wave, coord, which):
    sub_count, pol_count, row_count, width_two = subs.shape
    subgrid_len = width_two // 2
    blocks, slots = (coord.shape[0], coord.shape[2])
    real_part = subs[..., :subgrid_len]
    imag_part = subs[..., subgrid_len:]
    first_mat = jnp.concatenate([real_part, -imag_part], -1)
    second_mat = jnp.concatenate([imag_part, real_part], -1)
    stacked = jnp.stack([first_mat, second_mat], 2).reshape(-1, width_two)
    product = lax.dot_general(
        wave.reshape(blocks * slots, width_two),
        stacked,
        (((1,), (1,)), ((), ())),
        preferred_element_type=jnp.float32,
    )
    product = product.reshape(blocks, slots, sub_count, pol_count, 2, row_count)
    choose = (which[:, None] == jnp.arange(sub_count, dtype=jnp.int32)[None, :]).astype(jnp.float32)
    chosen = jnp.sum(product * choose[:, None, :, None, None, None], axis=2)
    cos_rows, sin_rows = row_phase(coord)
    cos_rows = cos_rows[:, :, None, :]
    sin_rows = sin_rows[:, :, None, :]
    real_y = chosen[:, :, :, 0, :]
    imag_y = chosen[:, :, :, 1, :]
    real_pred = jnp.sum(cos_rows * real_y - sin_rows * imag_y, -1)
    imag_pred = jnp.sum(cos_rows * imag_y + sin_rows * real_y, -1)
    result = jnp.stack([real_pred, imag_pred], -1).transpose(0, 2, 3, 1)
    return result / math.sqrt(ROWS * SS)


def grid(corr, wave, coord, which):
    blocks, pol_count, _, slots = corr.shape
    cos_rows, sin_rows = row_phase(coord)
    cos_rows = cos_rows[:, :, None, :]
    sin_rows = sin_rows[:, :, None, :]
    real_c = corr[:, :, 0, :].transpose(0, 2, 1)[..., None]
    imag_c = corr[:, :, 1, :].transpose(0, 2, 1)[..., None]
    real_z = cos_rows * real_c + sin_rows * imag_c
    imag_z = cos_rows * imag_c - sin_rows * real_c
    stacked = jnp.stack([real_z, imag_z], 3)
    choose = (which[:, None] == jnp.arange(SG_DEV, dtype=jnp.int32)[None, :]).astype(jnp.float32)
    weighted = (stacked[:, :, None] * choose[:, None, :, None, None, None]).astype(jnp.bfloat16)
    summed = lax.dot_general(
        wave.reshape(blocks * slots, 2 * SS),
        weighted.reshape(blocks * slots, -1),
        (((0,), (0,)), ((), ())),
        preferred_element_type=jnp.float32,
    )
    summed = summed.reshape(2 * SS, SG_DEV, pol_count, 2, ROWS)
    upper = summed[:SS]
    lower = summed[SS:]
    real_q = upper[:, :, :, 0, :] + lower[:, :, :, 1, :]
    imag_q = upper[:, :, :, 1, :] - lower[:, :, :, 0, :]
    result = jnp.concatenate([real_q, imag_q], 0).transpose(1, 2, 3, 0)
    return result / math.sqrt(ROWS * SS)


def on_device(
    facets, subgrid_offset, tile_subgrid, tile_count, vis_coord, stations, jones, observed
):
    facet_local = facets.shape[0]
    worker = lax.axis_index("work")
    forward, backward = transform_tables()
    facet_start = worker * facet_local
    offsets = subgrid_offset
    sums = lax.psum_scatter(
        to_subgrids(facets, facet_start, offsets, forward), "work", scatter_dimension=0, tiled=True
    )
    subs = lax.all_gather(sums.astype(jnp.bfloat16), "vis", axis=2, tiled=True)
    wave = wave_table(vis_coord)
    model = degrid(subs, wave, vis_coord, tile_subgrid)
    pol_count = model.shape[1]
    slot_total = model.shape[3]
    all_model = lax.all_gather(model.astype(jnp.bfloat16), "pol", axis=1, tiled=True).astype(
        model.dtype
    )
    left = jones_matrix(jones, stations, 0)
    right = jones_matrix(jones, stations, 1)
    apparent = apply_jones(left, right, all_model)
    first_pol = lax.axis_index("pol") * pol_count
    live = (jnp.arange(slot_total, dtype=jnp.int32)[None, :] < tile_count[:, None]).astype(
        jnp.float32
    )[:, None, None, :]
    residual_vis = (observed - lax.dynamic_slice_in_dim(apparent, first_pol, pol_count, 1)) * live
    all_resid = lax.all_gather(residual_vis.astype(jnp.bfloat16), "pol", axis=1, tiled=True).astype(
        residual_vis.dtype
    )
    corrected = lax.dynamic_slice_in_dim(
        adjoint_jones(left, right, all_resid), first_pol, pol_count, 1
    )
    partial_grid = grid(corrected, wave, vis_coord, tile_subgrid)
    grid_half = lax.psum_scatter(
        partial_grid.astype(jnp.bfloat16), "vis", scatter_dimension=2, tiled=True
    )
    offsets = subgrid_offset
    residual_image = to_facets(
        lax.all_gather(grid_half, "work", axis=0, tiled=True),
        offsets,
        facet_start,
        facet_local,
        backward,
    )
    return (residual_vis, residual_image)


def solution(mesh):
    in_specs = (
        P(("groups", "work"), "pol", "vis", None),
        P("groups"),
        P(("groups", "work", "vis")),
        P(("groups", "work", "vis")),
        P(("groups", "work", "vis"), None, None),
        P(("work", "vis"), None, None),
        P(None, "groups"),
        P(("groups", "work", "vis"), "pol", None, None),
    )
    out_specs = (
        P(("groups", "work", "vis"), "pol", None, None),
        P(("groups", "work"), "pol", "vis", None),
    )
    return jax.shard_map(
        on_device, mesh=mesh, in_specs=in_specs, out_specs=out_specs, check_vma=False
    )
```

profile of v0, /device:TPU:0, one launch (start us, length us, event | category | flops | bytes accessed | tf_op | source)
XLA Modules:
  0.0 219.8 jit_solution(14337042311997304026)
XLA Ops:
  7.2 8.5 %negate_convert_fusion.1 = (bf16[1024,512]{1,0:T(8,128)(2,1)S(1)}, bf16[1024,512]{1,0:T(8,128)(2,1)S(1)}) fusion(), kind=kLoop, calls=%fused_computation.62 | loop fusion | flops 8912896 | bytes 2097152 | tf_op jit(solution)/shard_map/convert.12
  15.8 8.6 %fusion.46 = bf16[1024,512]{1,0:T(8,128)(2,1)} fusion(), kind=kLoop, calls=%fused_computation.75 | loop fusion | flops 7864320 | bytes 1048576 | tf_op jit(solution)/shard_map/convert.15
  24.8 0.6 iota_convert_fusion
  26.0 0.6 fusion.73
  26.6 0.6 compare_and_fusion
  28.0 2.8 %multiply_cosine_fusion.2 = (f32[8,16,512]{2,1,0:T(8,128)S(1)}, f32[8,16,512]{2,1,0:T(8,128)}, f32[8,16,512]{2,1,0:T(8,128)S(1)}, f32[8,16,512]{2,1,0:T(8,128)S(1)}) fusion(s32[8,512]{1,0:T(8,128)S(1)} %iota_add_fusion, s32[16]{0:T(128)S(1)} %iota_add_fusion.1), kind=kLoop, calls=%fused_computation.94 | loop fusion | flops 983040 | bytes 1065024 | tf_op jit(solution)/shard_map/cos | solution.py:161
  30.8 1.1 subtract_convert_fusion
  32.0 4.5 %fusion.9 = f32[8,16,2,4,1024]{4,1,3,2,0:T(8,128)S(1)} fusion(bf16[8,16,2,4,1024]{4,1,3,2,0:T(8,128)(2,1)S(1)} %get-tuple-element.36, bf16[8,16,2,4,1024]{4,1,3,2,0:T(8,128)(2,1)S(1)} %get-tuple-element.35, bf16[1024,512]{1,0:T(8,128)(2,1)S(1)} %get-tuple-element.94, bf16[1024,512]{1,0:T(8,128)(2,1)S(1)} %get-tuple-element.93, bf16[1024,512]{1,0:T(8,128)(2,1)S(1)} %copy-done), kind=kOutput, calls=%fused_computation.16 | convolution fusion | flops 4320133120 | bytes 11534336 | tf_op jit(solution)/shard_map/dot_general | solution.py:133
  36.5 1.3 subtract_reduce_fusion.1
  37.9 25.8 %all-reduce.6 = bf16[8,2,4,1024]{3,2,1,0:T(4,128)(2,1)S(1)} all-reduce(f32[8,2,4,1024]{3,2,1,0:T(4,128)S(1)} %maximum_multiply_fusion.1), channel_id=2, replica_groups=mesh['groups'=2,'work'=4,'pol'=2,'vis'=2] {'work'}, use_global_device_ids=true, to_apply=%region_2.4.clone | all-reduce | flops 65536 | bytes 393216
  63.8 0.6 dynamic-slice
  65.1 2.0 all_gather.12
  67.4 31.3 %fusion = (bf16[4,1024,512]{2,1,0:T(8,128)(2,1)S(1)}, bf16[4,1024,512]{2,1,0:T(8,128)(2,1)S(1)}) fusion(f32[512]{0:T(512)S(1)} %copy-done.6, f32[4,1024]{1,0:T(4,128)S(1)} %get-tuple-element.91), kind=kLoop, calls=%fused_computation.6 | loop fusion | flops 6291456 | bytes 8407040 | tf_op jit(solution)/shard_map/convert.18
  99.3 2.8 %fusion.42 = f32[4,1024,2,2,8]{1,4,3,2,0:T(8,128)S(1)} fusion(bf16[4,1024,512]{2,1,0:T(8,128)(2,1)S(1)} %get-tuple-element.76, bf16[4,1024,512]{2,1,0:T(8,128)(2,1)S(1)} %get-tuple-element.75, f32[4,2]{1,0:T(4,128)S(1)} %fusion.75, bf16[2,2,1,8,1024]{4,3,2,1,0:T(8,128)(2,1)S(1)} %get-tuple-element.70, bf16[2,2,1,8,1024]{4,3,2,1,0:T(8,128)(2,1)S(1)} %get-tuple-element.69), kind=kOutput, calls=%fused_computation.69 | convolution fusion | flops 554303488 | bytes 9044000 | tf_op jit(solution)/shard_map/dot_general | solution.py:208
  102.4 4.6 %all_gather.13 = bf16[4,4,2,1024]{3,0,2,1:T(4,128)(2,1)S(1)} all-gather(bf16[4,2,2,1024]{3,0,2,1:T(4,128)(2,1)S(1)} %copy.85), channel_id=1, replica_groups=mesh['groups'=2,'work'=4,'pol'=2,'vis'=2] {'pol'}, dimensions={1}, use_global_device_ids=true | all-gather | bytes 98304 | tf_op jit(solution)/shard_map/all_gather | solution.py:271
  107.2 10.8 %gather_fusion.1 = f32[4096,8]{1,0:T(8,128)S(1)} fusion(f32[8,512]{0,1:T(8,128)S(1)} %copy.76, s32[4096]{0:T(1024)S(1)} %bitcast_clamp_fusion), kind=kCustom, calls=%fused_computation.1.clone | custom fusion | bytes 278528 | tf_op jit(solution)/shard_map/jit(_take)/gather | solution.py:31
  118.6 10.8 %gather_fusion = f32[4096,8]{1,0:T(8,128)S(1)} fusion(f32[8,512]{0,1:T(8,128)S(1)} %copy.76, s32[4096]{0:T(1024)S(1)} %bitcast_clamp_fusion.1), kind=kCustom, calls=%fused_computation.clone | custom fusion | bytes 278528 | tf_op jit(solution)/shard_map/jit(_take)/gather | solution.py:31
  130.4 0.9 fusion.80
  131.3 4.6 %all_gather.14 = bf16[4,4,2,1024]{3,0,2,1:T(4,128)(2,1)S(1)} all-gather(bf16[4,2,2,1024]{3,0,2,1:T(4,128)(2,1)S(1)} %get-tuple-element.23), channel_id=1, replica_groups=mesh['groups'=2,'work'=4,'pol'=2,'vis'=2] {'pol'}, dimensions={1}, use_global_device_ids=true | all-gather | bytes 98304 | tf_op jit(solution)/shard_map/all_gather | solution.py:282
  137.2 31.4 %fusion.2 = (bf16[4096,512]{1,0:T(8,128)(2,1)S(1)}, bf16[4096,512]{1,0:T(8,128)(2,1)S(1)}) fusion(f32[512]{0:T(512)S(1)} %copy-done.6, f32[4096]{0:T(1024)S(1)} %bitcast.721), kind=kLoop, calls=%fused_computation.8 | loop fusion | flops 6291456 | bytes 8407040 | tf_op jit(solution)/shard_map/convert.8
  168.7 1.5 fusion.4
  170.3 0.6 fusion.52
  170.9 8.5 %negate_convert_fusion = (bf16[512,1024]{1,0:T(8,128)(2,1)S(1)}, bf16[512,1024]{1,0:T(8,128)(2,1)S(1)}) fusion(), kind=kLoop, calls=%fused_computation.54 | loop fusion | flops 8912896 | bytes 2097152 | tf_op jit(solution)/shard_map/convert.5
  179.4 7.8 %fusion.44 = bf16[512,1024]{1,0:T(8,128)(2,1)S(1)} fusion(), kind=kLoop, calls=%fused_computation.72 | loop fusion | flops 7864320 | bytes 1048576 | tf_op jit(solution)/shard_map/convert.2
  187.3 0.7 dynamic-slice.2
  187.9 0.7 copy.96
  189.3 0.9 constant_dynamic-slice_fusion
  190.1 13.6 %all_gather.15 = bf16[8,2,4,1024]{3,2,1,0:T(4,128)(2,1)S(1)} all-gather(bf16[2,2,4,1024]{3,2,1,0:T(4,128)(2,1)S(1)} %constant_dynamic-slice_fusion), channel_id=1, replica_groups=mesh['groups'=2,'work'=4,'pol'=2,'vis'=2] {'work'}, dimensions={0}, use_global_device_ids=true | all-gather | bytes 163840 | tf_op jit(solution)/shard_map/all_gather | solution.py:294
  203.7 1.7 subtract_convert_fusion.1
  205.5 4.5 %fusion.19 = f32[8,16,2,4,2048]{4,1,3,2,0:T(8,128)S(1)} fusion(bf16[512,1024]{1,0:T(8,128)(2,1)S(1)} %get-tuple-element.96, bf16[512,1024]{1,0:T(8,128)(2,1)S(1)} %fusion.44, bf16[512,1024]{1,0:T(8,128)(2,1)S(1)} %get-tuple-element.95, bf16[8,16,2,4,512]{4,1,3,2,0:T(8,128)(2,1)S(1)} %get-tuple-element.38, bf16[8,16,2,4,512]{4,1,3,2,0:T(8,128)(2,1)S(1)} %get-tuple-element.37), kind=kOutput, calls=%fused_computation.28 | convolution fusion | flops 4315938816 | bytes 13631488 | tf_op jit(solution)/shard_map/dot_general | solution.py:168
  210.0 1.2 subtract_reduce_fusion
  211.3 1.6 copy.97
  (96 shorter events, 6.1 us)
Async XLA Ops:
  7.2 17.2 %copy-start.10 = (s32[8]{0:T(128)S(1)}, s32[8]{0:T(128)}, u32[]{:S(2)}) copy-start(s32[8]{0:T(128)} %param.11) | copy-start | bytes 100
  7.2 18.8 %copy-start.4 = (s32[4,2,1024]{2,1,0:T(2,128)S(1)}, s32[4,2,1024]{2,1,0:T(2,128)}, u32[]{:S(2)}) copy-start(s32[4,2,1024]{2,1,0:T(2,128)} %param.15) | copy-start | bytes 98308
  7.2 20.0 %copy-start.1 = (bf16[16,2,4,2048]{3,2,1,0:T(4,128)(2,1)S(1)}, bf16[16,2,4,2048]{3,2,1,0:T(4,128)(2,1)}, u32[]{:S(2)}) copy-start(bf16[16,2,4,2048]{3,2,1,0:T(4,128)(2,1)} %param.10) | copy-start | bytes 1572868
  7.2 182.1 %all-reduce.5.cloned.1.call-start = ((), (), s32[]{:S(2)}) async-start(), calls=%async_computation | async-start | bytes 131072
  30.7 1.2 copy-start
  36.5 27.3 %copy-start.15 = (u32[32]{0:T(128)S(1)}, u32[32]{0:T(128)}, u32[]{:S(2)}) copy-start(u32[32]{0:T(128)} %constant.114) | copy-start | bytes 388
  36.5 30.7 %copy-start.5 = (f32[4,2,1024]{2,1,0:T(2,128)S(1)}, f32[4,2,1024]{2,1,0:T(2,128)}, u32[]{:S(2)}) copy-start(f32[4,2,1024]{2,1,0:T(2,128)} %param.14) | copy-start | bytes 98308
  36.5 30.8 %copy-start.12 = (s32[4]{0:T(128)S(1)}, s32[4]{0:T(128)}, u32[]{:S(2)}) copy-start(s32[4]{0:T(128)} %param.12) | copy-start | bytes 52
  36.5 30.8 %copy-start.6 = (f32[512]{0:T(512)S(1)}, f32[512]{0:T(512)}, u32[]{:S(2)}) copy-start(f32[512]{0:T(512)} %iota_convert_fusion) | copy-start | bytes 6148
  67.4 31.3 %copy-start.11 = (f32[8]{0:T(128)S(1)}, f32[8]{0:T(128)}, u32[]{:S(2)}) copy-start(f32[8]{0:T(128)} %iota_convert_fusion.1) | copy-start | bytes 100
  99.3 7.7 %copy-start.3 = (s32[1,8,4,128]{3,2,1,0:T(4,128)S(1)}, s32[1,8,4,128]{3,2,1,0:T(4,128)}, u32[]{:S(2)}) copy-start(s32[1,8,4,128]{3,2,1,0:T(4,128)} %get-tuple-element.90) | copy-start | bytes 49156
  99.3 7.7 %copy-start.9 = (f32[8,512]{1,0:T(8,128)S(1)}, f32[8,512]{1,0:T(8,128)}, u32[]{:S(2)}) copy-start(f32[8,512]{1,0:T(8,128)} %param.16) | copy-start | bytes 49156
  102.3 16.2 %copy-start.2 = (s32[1,8,4,128]{3,2,1,0:T(4,128)S(1)}, s32[1,8,4,128]{3,2,1,0:T(4,128)}, u32[]{:S(2)}) copy-start(s32[1,8,4,128]{3,2,1,0:T(4,128)} %get-tuple-element.89) | copy-start | bytes 49156
  118.5 11.4 %copy-start.8 = (pred[4,1024]{1,0:T(4,128)(4,1)S(1)}, pred[4,1024]{1,0:T(4,128)(4,1)}, u32[]{:S(2)}) copy-start(pred[4,1024]{1,0:T(4,128)(4,1)} %get-tuple-element.87) | copy-start | bytes 12292
  118.5 11.5 %copy-start.7 = (pred[4,1024]{1,0:T(4,128)(4,1)S(1)}, pred[4,1024]{1,0:T(4,128)(4,1)}, u32[]{:S(2)}) copy-start(pred[4,1024]{1,0:T(4,128)(4,1)} %get-tuple-element.88) | copy-start | bytes 12292
  118.6 11.6 %copy-start.13 = (s32[4]{0:T(128)S(1)}, s32[4]{0:T(128)}, u32[]{:S(2)}) copy-start(s32[4]{0:T(128)} %param.13) | copy-start | bytes 52
  170.2 17.1 %copy-start.14 = (u32[32]{0:T(128)S(1)}, u32[32]{0:T(128)}, u32[]{:S(2)}) copy-start(u32[32]{0:T(128)} %constant.118) | copy-start | bytes 388
Sparse Core Ops, SparseCore 0:
  171.0 16.2 all-reduce.4
where the time goes:
time: 220 us
  other arithmetic  111 us (50%)
  blocking collectives  50.6 us (23%)
  local copies, waits for them, and re-layouts  28.9 us (13%)
  between operations  16 us (7%)
  matrix products  13.4 us (6%)
    another operation x8, other arithmetic  99.1 us
    unnamed x1, blocking collectives  25.8 us
    gather x4, local copies, waits for them, and re-layouts, jones_matrix(): picked = jnp.take(table, pairs[:, column, :], axis=1)  22.7 us
    all_gather x1, blocking collectives, on_device(): lax.all_gather(grid_half, 'work', axis=0, tiled=True)  13.6 us
    unnamed x41, local copies, waits for them, and re-layouts  4.9 us
    all_gather x1, blocking collectives, on_device(): lax.all_gather(model.astype(jnp.bfloat16), 'pol', axis=1, tiled=True)  4.58 us
    all_gather x1, blocking collectives, on_device(): lax.all_gather(residual_vis.astype(jnp.bfloat16), 'pol', axis=1, tiled=True)  4.58 us
    dot_general x1, matrix products, to_facets(): jnp.dot(rotated.reshape(-1, 2 * subgrid_len), backward, preferred_element...  4.53 us
  transfers between devices with their start and end apart: 1, of which 0 were waited for; matrix products, arithmetic and copies ran while one was open for 8% of the time, Pallas kernels for 0%

commit v1 on v0

v1 whole, which is shorter than its diff:
```python
import functools
import math

import jax
import jax.numpy as jnp
from jax import lax
from jax.experimental import pallas as pl
from jax.experimental.pallas import tpu as pltpu
from jax.sharding import PartitionSpec as P

SS = 512
STEP = 32
MESH = pl.DeviceIdType.MESH
F32 = jnp.float32
BF16 = jnp.bfloat16
VMEM = pl.BlockSpec(memory_space=pltpu.VMEM)
SMEM = pl.BlockSpec(memory_space=pltpu.SMEM)
LIMIT = 60 * 1024 * 1024


def sincos(turns):
    y = (turns - jnp.floor(turns + 0.5)) * (0.5 * math.pi)
    q = y * y
    s = y * (1.0 + q * (-1 / 6 + q * (1 / 120 + q * (-1 / 5040 + q * (1 / 362880)))))
    c = 1.0 + q * (-1 / 2 + q * (1 / 24 + q * (-1 / 720 + q * (1 / 40320))))
    for _ in range(2):
        s, c = 2.0 * s * c, 1.0 - 2.0 * s * s
    return s, c


def iota(shape, axis):
    return lax.broadcasted_iota(jnp.int32, shape, axis)


def int_turns(product, length):
    return lax.rem(product, length).astype(F32) * (1.0 / length)


def fill_table(cos_ref, sin_ref, image_len):
    rows, cols = cos_ref.shape
    coarse = rows // STEP
    sa, ca = sincos(-int_turns(iota((coarse, cols), 0) * STEP * iota((coarse, cols), 1), image_len))
    sb, cb = sincos(-int_turns(iota((STEP, cols), 0) * iota((STEP, cols), 1), image_len))
    for a in range(coarse):
        s, c = sa[a : a + 1], ca[a : a + 1]
        cos_ref[a * STEP : (a + 1) * STEP, :] = (c * cb - s * sb).astype(BF16)
        sin_ref[a * STEP : (a + 1) * STEP, :] = (s * cb + c * sb).astype(BF16)


def forward_kernel(
    facet_total, per_facet, chunk, off_ref, fac_ref, out_ref, cos_ref, sin_ref, re_ref, im_ref
):
    rows, width_two = fac_ref.shape
    cells = width_two // 2
    count = rows // per_facet
    image_len = facet_total * cells
    step = pl.program_id(0)

    @pl.when(step == 0)
    def _():
        fill_table(cos_ref, sin_ref, image_len)

    start = lax.axis_index("work") * count
    for i in range(chunk):
        offset = off_ref[step * chunk + i]
        s, c = sincos(-int_turns(iota((1, cells), 1) * offset, image_len))
        real = fac_ref[:, :cells].astype(F32)
        imag = fac_ref[:, cells:].astype(F32)
        re_ref[i * rows : (i + 1) * rows, :] = (real * c - imag * s).astype(BF16)
        im_ref[i * rows : (i + 1) * rows, :] = (real * s + imag * c).astype(BF16)
    dot = functools.partial(jnp.dot, preferred_element_type=F32)
    real_spec = dot(re_ref[...], cos_ref[...]) - dot(im_ref[...], sin_ref[...])
    imag_spec = dot(re_ref[...], sin_ref[...]) + dot(im_ref[...], cos_ref[...])
    scale = 1.0 / math.sqrt(image_len)
    for i in range(chunk):
        offset = off_ref[step * chunk + i]
        ids = start + iota((count, SS), 0)
        s, c = sincos(-int_turns(ids * (offset + iota((count, SS), 1)), facet_total))
        real = imag = 0.0
        for f in range(count):
            first = i * rows + f * per_facet
            a = real_spec[first : first + per_facet]
            b = imag_spec[first : first + per_facet]
            real += a * c[f : f + 1] - b * s[f : f + 1]
            imag += a * s[f : f + 1] + b * c[f : f + 1]
        out_ref[i, :, :SS] = (real * scale).astype(BF16)
        out_ref[i, :, SS:] = (imag * scale).astype(BF16)


def chunk_of(number, rows):
    chunk = max(1, min(number, 256 // rows))
    while number % chunk:
        chunk -= 1
    return chunk


def forward(facets, offsets, facet_total):
    count, pols, lines, width_two = facets.shape
    number = offsets.shape[0]
    rows = count * pols * lines
    cells = width_two // 2
    chunk = chunk_of(number, rows)
    return pl.pallas_call(
        functools.partial(forward_kernel, facet_total, pols * lines, chunk),
        out_shape=jax.ShapeDtypeStruct((number, pols * lines, 2 * SS), BF16),
        grid=(number // chunk,),
        in_specs=[SMEM, pl.BlockSpec((rows, width_two), lambda i: (0, 0))],
        out_specs=pl.BlockSpec((chunk, pols * lines, 2 * SS), lambda i: (i, 0, 0)),
        scratch_shapes=[
            pltpu.VMEM((cells, SS), BF16),
            pltpu.VMEM((cells, SS), BF16),
            pltpu.VMEM((chunk * rows, cells), BF16),
            pltpu.VMEM((chunk * rows, cells), BF16),
        ],
        compiler_params=pltpu.CompilerParams(vmem_limit_bytes=LIMIT),
        name="forward",
    )(offsets, facets.reshape(rows, width_two))


def backward_kernel(
    facet_total, count, chunk, off_ref, grid_ref, out_ref, cos_ref, sin_ref, re_ref, im_ref
):
    per_facet = grid_ref.shape[1]
    cells = cos_ref.shape[1]
    rows = count * per_facet
    image_len = facet_total * cells
    step = pl.program_id(0)

    @pl.when(step == 0)
    def _():
        fill_table(cos_ref, sin_ref, image_len)

    start = lax.axis_index("work") * count
    for i in range(chunk):
        offset = off_ref[step * chunk + i]
        ids = start + iota((count, SS), 0)
        s, c = sincos(int_turns(ids * (offset + iota((count, SS), 1)), facet_total))
        real = grid_ref[i, :, :SS].astype(F32)
        imag = grid_ref[i, :, SS:].astype(F32)
        for f in range(count):
            first = i * rows + f * per_facet
            sf, cf = s[f : f + 1], c[f : f + 1]
            re_ref[first : first + per_facet, :] = (real * cf - imag * sf).astype(BF16)
            im_ref[first : first + per_facet, :] = (real * sf + imag * cf).astype(BF16)
    dot = functools.partial(jnp.dot, preferred_element_type=F32)
    real_img = dot(re_ref[...], cos_ref[...]) + dot(im_ref[...], sin_ref[...])
    imag_img = dot(im_ref[...], cos_ref[...]) - dot(re_ref[...], sin_ref[...])
    scale = 1.0 / math.sqrt(image_len)
    real_sum = imag_sum = 0.0
    for i in range(chunk):
        offset = off_ref[step * chunk + i]
        s, c = sincos(int_turns(iota((1, cells), 1) * offset, image_len))
        s, c = s * scale, c * scale
        a = real_img[i * rows : (i + 1) * rows]
        b = imag_img[i * rows : (i + 1) * rows]
        real_sum += a * c - b * s
        imag_sum += a * s + b * c

    @pl.when(step == 0)
    def _():
        out_ref[:, :cells] = real_sum
        out_ref[:, cells:] = imag_sum

    @pl.when(step > 0)
    def _():
        out_ref[:, :cells] += real_sum
        out_ref[:, cells:] += imag_sum


def backward(grids, offsets, facet_total, count, cells):
    number, per_facet, _ = grids.shape
    rows = count * per_facet
    chunk = chunk_of(number, rows)
    return pl.pallas_call(
        functools.partial(backward_kernel, facet_total, count, chunk),
        out_shape=jax.ShapeDtypeStruct((rows, 2 * cells), F32),
        grid=(number // chunk,),
        in_specs=[SMEM, pl.BlockSpec((chunk, per_facet, 2 * SS), lambda i: (i, 0, 0))],
        out_specs=pl.BlockSpec((rows, 2 * cells), lambda i: (0, 0)),
        scratch_shapes=[
            pltpu.VMEM((SS, cells), BF16),
            pltpu.VMEM((SS, cells), BF16),
            pltpu.VMEM((chunk * rows, SS), BF16),
            pltpu.VMEM((chunk * rows, SS), BF16),
        ],
        compiler_params=pltpu.CompilerParams(vmem_limit_bytes=LIMIT),
        name="backward",
    )(offsets, grids)


def cmul(a, b):
    return (a[0] * b[0] - a[1] * b[1], a[0] * b[1] + a[1] * b[0])


def conj(a):
    return (a[0], -a[1])


def cadd(a, b):
    return (a[0] + b[0], a[1] + b[1])


def pick(flag, a, b):
    return (jnp.where(flag, a[0], b[0]), jnp.where(flag, a[1], b[1]))


def visibility_kernel(
    pols, which_ref, count_ref, coord_ref, stat_ref, jones_ref, obs_ref, subs_ref,
    resid_ref, grid_ref, wave_ref, stack_ref, acc_ref, hot_ref, weight_ref,
):
    chips, halves, subs, _, width = subs_ref.shape
    lines = subs_ref.shape[3] // pols
    all_rows = lines * halves
    total = chips * pols
    slots = coord_ref.shape[2]
    step = pl.program_id(0)

    @pl.when(step == 0)
    def _():
        acc_ref[...] = jnp.zeros_like(acc_ref)
        for g in range(subs):
            for p in range(total):
                for h in range(halves):
                    at = (p % pols) * lines
                    both = subs_ref[p // pols, h, g, at : at + lines, :].astype(F32)
                    real, imag = both[:, :SS], both[:, SS:]
                    row = p * all_rows + h * lines
                    low = total * all_rows + row
                    stack_ref[g, row : row + lines, :SS] = real
                    stack_ref[g, row : row + lines, SS:] = -imag
                    stack_ref[g, low : low + lines, :SS] = imag
                    stack_ref[g, low : low + lines, SS:] = real

    coord = coord_ref[0]
    m, l = coord[1:2], coord[0:1]
    coarse = SS // STEP
    sa, ca = sincos(iota((coarse, slots), 0).astype(F32) * STEP * m)
    sb, cb = sincos(iota((STEP, slots), 0).astype(F32) * m)
    for a in range(coarse):
        s, c = sa[a : a + 1], ca[a : a + 1]
        wave_ref[a * STEP : (a + 1) * STEP, :] = (c * cb - s * sb).astype(BF16)
        wave_ref[SS + a * STEP : SS + (a + 1) * STEP, :] = (s * cb + c * sb).astype(BF16)
    sr, cr = sincos(iota((all_rows, slots), 0).astype(F32) * l)

    which = which_ref[step]
    chosen = stack_ref[0]
    for g in range(1, subs):
        chosen = jnp.where(which == g, stack_ref[g], chosen)
    product = jnp.dot(chosen.astype(BF16), wave_ref[...], preferred_element_type=F32)
    scale = 1.0 / math.sqrt(all_rows * SS)
    model = []
    for p in range(total):
        low = (total + p) * all_rows
        y_re = product[p * all_rows : (p + 1) * all_rows]
        y_im = product[low : low + all_rows]
        re = jnp.sum(cr * y_re - sr * y_im, axis=0, keepdims=True) * scale
        im = jnp.sum(cr * y_im + sr * y_re, axis=0, keepdims=True) * scale
        model.append((re, im))

    table = jones_ref[...]
    high = table.astype(BF16)
    rest = table - high.astype(F32)
    middle = rest.astype(BF16)
    low_part = (rest - middle.astype(F32)).astype(BF16)
    parts = jnp.concatenate([high, middle, low_part], 0)
    entries = table.shape[0]
    sides = []
    for side in range(2):
        hot = iota((table.shape[1], slots), 0) == stat_ref[0, side : side + 1, :]
        hot_ref[...] = jnp.where(hot, 1.0, 0.0).astype(BF16)
        got = jnp.dot(parts, hot_ref[...], preferred_element_type=F32)
        got = (got[2 * entries :] + got[entries : 2 * entries]) + got[:entries]
        half = entries // 2
        sides.append([[(got[2 * i + k : 2 * i + k + 1], got[half + 2 * i + k : half + 2 * i + k + 1])
                       for k in range(2)] for i in range(2)])
    left, right = sides

    bright = [[model[2 * i + k] for k in range(2)] for i in range(2)]
    inner = [[cadd(cmul(left[i][0], bright[0][k]), cmul(left[i][1], bright[1][k]))
              for k in range(2)] for i in range(2)]
    outer = [[cadd(cmul(inner[i][0], conj(right[k][0])), cmul(inner[i][1], conj(right[k][1])))
              for k in range(2)] for i in range(2)]
    live = iota((1, slots), 1) < count_ref[step]
    resid = []
    for p in range(total):
        at = (p % pols) * 2
        seen = (obs_ref[p // pols, 0, at : at + 1, :], obs_ref[p // pols, 0, at + 1 : at + 2, :])
        got = outer[p // 2][p % 2]
        resid.append((jnp.where(live, seen[0] - got[0], 0.0), jnp.where(live, seen[1] - got[1], 0.0)))
    mine = lax.axis_index("pol") * pols
    for j in range(pols):
        p = mine + j
        own = resid[0]
        for other in range(1, total):
            own = pick(p == other, resid[other], own)
        resid_ref[0, 2 * j : 2 * j + 1, :] = own[0]
        resid_ref[0, 2 * j + 1 : 2 * j + 2, :] = own[1]
        first, second = p < 2, lax.rem(p, 2) == 0
        l0 = conj(pick(first, left[0][0], left[0][1]))
        l1 = conj(pick(first, left[1][0], left[1][1]))
        r0 = pick(second, right[0][0], right[0][1])
        r1 = pick(second, right[1][0], right[1][1])
        t0 = cadd(cmul(l0, resid[0]), cmul(l1, resid[2]))
        t1 = cadd(cmul(l0, resid[1]), cmul(l1, resid[3]))
        cre, cim = cadd(cmul(t0, r0), cmul(t1, r1))
        row = 2 * j * all_rows
        weight_ref[row : row + all_rows, :] = cr * cre + sr * cim
        weight_ref[row + all_rows : row + 2 * all_rows, :] = cr * cim - sr * cre
    summed = lax.dot_general(
        weight_ref[...].astype(BF16), wave_ref[...], (((1,), (1,)), ((), ())),
        preferred_element_type=F32,
    )
    for g in range(subs):
        acc_ref[g] += jnp.where(which == g, summed, 0.0)

    @pl.when(step == pl.num_programs(0) - 1)
    def _():
        for g in range(subs):
            for j in range(pols):
                row = 2 * j * all_rows
                real_z = acc_ref[g, row : row + all_rows, :]
                imag_z = acc_ref[g, row + all_rows : row + 2 * all_rows, :]
                real = ((real_z[:, :SS] + imag_z[:, SS:]) * scale).astype(BF16)
                imag = ((imag_z[:, :SS] - real_z[:, SS:]) * scale).astype(BF16)
                for h in range(halves):
                    cut = slice(h * lines, (h + 1) * lines)
                    grid_ref[h, g, j * lines : (j + 1) * lines, :SS] = real[cut]
                    grid_ref[h, g, j * lines : (j + 1) * lines, SS:] = imag[cut]


def visibilities(which, counts, coord, stations, jones, seen, subs, pols):
    blocks, _, slots = coord.shape
    chips, halves, sub_count, wide, width = subs.shape
    rows = halves * wide // pols
    total = chips * pols
    return pl.pallas_call(
        functools.partial(visibility_kernel, pols),
        out_shape=(
            jax.ShapeDtypeStruct((blocks, 2 * pols, slots), F32),
            jax.ShapeDtypeStruct((halves, sub_count, wide, width), BF16),
        ),
        grid=(blocks,),
        in_specs=[
            SMEM,
            SMEM,
            pl.BlockSpec((1, 2, slots), lambda i: (i, 0, 0)),
            pl.BlockSpec((1, 2, slots), lambda i: (i, 0, 0)),
            pl.BlockSpec(jones.shape, lambda i: (0, 0)),
            pl.BlockSpec((chips, 1, 2 * pols, slots), lambda i: (0, i, 0, 0)),
            pl.BlockSpec(subs.shape, lambda i: (0, 0, 0, 0, 0)),
        ],
        out_specs=(
            pl.BlockSpec((1, 2 * pols, slots), lambda i: (i, 0, 0)),
            pl.BlockSpec((halves, sub_count, wide, width), lambda i: (0, 0, 0, 0)),
        ),
        scratch_shapes=[
            pltpu.VMEM((2 * SS, slots), BF16),
            pltpu.VMEM((sub_count, 2 * total * rows, width), F32),
            pltpu.VMEM((sub_count, 2 * pols * rows, width), F32),
            pltpu.VMEM((jones.shape[1], slots), BF16),
            pltpu.VMEM((2 * pols * rows, slots), F32),
        ],
        compiler_params=pltpu.CompilerParams(vmem_limit_bytes=LIMIT),
        name="visibilities",
    )(which, counts, coord, stations, jones, seen, subs)


def send(src, dst, send_sem, recv_sem, device):
    copy = pltpu.make_async_remote_copy(
        src_ref=src, dst_ref=dst, send_sem=send_sem, recv_sem=recv_sem,
        device_id=device, device_id_type=MESH,
    )
    copy.start()
    return copy


def meet(devices):
    barrier = pltpu.get_barrier_semaphore()
    for device in devices:
        pl.semaphore_signal(barrier, inc=1, device_id=device, device_id_type=MESH)
    pl.semaphore_wait(barrier, len(devices))


def ahead(name, size, hop):
    return lax.rem(lax.axis_index(name) + hop, size)


def join_kernel(
    work, pol, vis, part_ref, obs_ref, subs_ref, seen_ref,
    land_ref, s_work, r_work, s_out, r_out, s_obs, r_obs,
):
    me, my_pol, my_vis = (lax.axis_index(n) for n in ("work", "pol", "vis"))
    peers = [{"work": ahead("work", work, d)} for d in range(1, work)]
    mates = [
        {"pol": ahead("pol", pol, a), "vis": ahead("vis", vis, b)}
        for a in range(pol) for b in range(vis) if a + b > 0
    ]
    meet(peers + mates)
    copies = [
        send(part_ref.at[ahead("work", work, d)], land_ref.at[d - 1], s_work.at[d - 1],
             r_work.at[d - 1], peers[d - 1])
        for d in range(1, work)
    ]
    seen_copies = [
        send(obs_ref, seen_ref.at[my_pol], s_obs.at[a - 1], r_obs.at[a - 1],
             {"pol": ahead("pol", pol, a)})
        for a in range(1, pol)
    ]
    seen_ref[my_pol] = obs_ref[...]
    total = part_ref[me].astype(F32)
    for d, copy in enumerate(copies):
        copy.wait()
        total += land_ref[d].astype(F32)
    subs_ref[my_pol, my_vis] = total.astype(BF16)
    own = subs_ref.at[my_pol, my_vis]
    spread = [send(own, own, s_out.at[i], r_out.at[i], mate) for i, mate in enumerate(mates)]
    for copy in seen_copies + spread:
        copy.wait()


def join(part, seen, sizes):
    work, pol, vis = sizes
    number, wide, width = part.shape
    mates = pol * vis - 1
    dma = pltpu.SemaphoreType.DMA
    return pl.pallas_call(
        functools.partial(join_kernel, work, pol, vis),
        out_shape=(
            jax.ShapeDtypeStruct((pol, vis, number // work, wide, width), BF16),
            jax.ShapeDtypeStruct((pol,) + seen.shape, F32),
        ),
        in_specs=[VMEM, VMEM],
        out_specs=(VMEM, VMEM),
        scratch_shapes=[
            pltpu.VMEM((work - 1, number // work, wide, width), BF16),
            dma((work - 1,)), dma((work - 1,)), dma((mates,)), dma((mates,)),
            dma((pol - 1,)), dma((pol - 1,)),
        ],
        compiler_params=pltpu.CompilerParams(
            collective_id=0, has_side_effects=True, vmem_limit_bytes=LIMIT
        ),
        name="join",
    )(part.reshape(work, number // work, wide, width), seen)


def spread_kernel(work, vis, part_ref, out_ref, land_ref, s_vis, r_vis, s_work, r_work):
    me, my_vis = lax.axis_index("work"), lax.axis_index("vis")
    peers = [{"work": ahead("work", work, d)} for d in range(1, work)]
    mates = [{"vis": ahead("vis", vis, b)} for b in range(1, vis)]
    meet(peers + mates)
    copies = [
        send(part_ref.at[ahead("vis", vis, b)], land_ref.at[b - 1], s_vis.at[b - 1],
             r_vis.at[b - 1], mates[b - 1])
        for b in range(1, vis)
    ]
    total = part_ref[my_vis].astype(F32)
    for b, copy in enumerate(copies):
        copy.wait()
        total += land_ref[b].astype(F32)
    out_ref[me] = total.astype(BF16)
    own = out_ref.at[me]
    for copy in [send(own, own, s_work.at[d], r_work.at[d], peers[d]) for d in range(work - 1)]:
        copy.wait()


def spread(part, sizes):
    work, pol, vis = sizes
    _, subs, wide, width = part.shape
    dma = pltpu.SemaphoreType.DMA
    return pl.pallas_call(
        functools.partial(spread_kernel, work, vis),
        out_shape=jax.ShapeDtypeStruct((work, subs, wide, width), BF16),
        in_specs=[VMEM],
        out_specs=VMEM,
        scratch_shapes=[
            pltpu.VMEM((vis - 1, subs, wide, width), BF16),
            dma((vis - 1,)), dma((vis - 1,)), dma((work - 1,)), dma((work - 1,)),
        ],
        compiler_params=pltpu.CompilerParams(
            collective_id=1, has_side_effects=True, vmem_limit_bytes=LIMIT
        ),
        name="spread",
    )(part)


def on_device(
    sizes, facets, subgrid_offset, tile_subgrid, tile_count, vis_coord, stations, jones, observed
):
    count, pols, lines, width_two = facets.shape
    blocks, _, _, slots = observed.shape
    facet_total = count * sizes[0]
    part = forward(facets, subgrid_offset, facet_total)
    subs, seen = join(part, observed.reshape(blocks, 2 * pols, slots), sizes)
    resid, grid_part = visibilities(
        tile_subgrid, tile_count, vis_coord, stations, jones, seen, subs, pols
    )
    grids = spread(grid_part, sizes)
    number = subgrid_offset.shape[0]
    image = backward(
        grids.reshape(number, pols * lines, 2 * SS), subgrid_offset, facet_total, count,
        width_two // 2,
    )
    return resid.reshape(observed.shape), image.reshape(facets.shape)


def solution(mesh):
    sizes = tuple(mesh.shape[name] for name in ("work", "pol", "vis"))
    in_specs = (
        P(("groups", "work"), "pol", "vis", None),
        P("groups"),
        P(("groups", "work", "vis")),
        P(("groups", "work", "vis")),
        P(("groups", "work", "vis"), None, None),
        P(("work", "vis"), None, None),
        P(None, "groups"),
        P(("groups", "work", "vis"), "pol", None, None),
    )
    out_specs = (
        P(("groups", "work", "vis"), "pol", None, None),
        P(("groups", "work"), "pol", "vis", None),
    )
    return jax.shard_map(
        functools.partial(on_device, sizes),
        mesh=mesh, in_specs=in_specs, out_specs=out_specs, check_vma=False,
    )
```

time: 220 us -> 59.8 us (0.27)
  other arithmetic: 111 us -> 0 us
  Pallas kernels: 0 us -> 51.2 us
  blocking collectives: 50.6 us -> 0 us
  local copies, waits for them, and re-layouts: 28.9 us -> 7.49 us
  between operations: 16 us -> 0.65 us
  matrix products: 13.4 us -> 0 us
    another operation x19 -> x0, other arithmetic: 99.2 us -> none
    pallas_call x0 -> x5, Pallas kernels: none -> 51.2 us  [the longest x1 13.6 us: join(): pl.pallas_call(functools.partial(join_kernel, work, pol, vis), out_shape=...]
    unnamed x1 -> x0, blocking collectives: 25.8 us -> none
    all_gather x4 -> x0, blocking collectives: 24.8 us -> none  [the longest x1 13.6 us: on_device(): lax.all_gather(grid_half, 'work', axis=0, tiled=True)]
    gather x4 -> x0, local copies, waits for them, and re-layouts: 22.7 us -> none  [jones_matrix(): picked = jnp.take(table, pairs[:, column, :], axis=1)]
    dot_general x4 -> x0, matrix products: 13.4 us -> none  [the longest x1 4.53 us: to_facets(): jnp.dot(rotated.reshape(-1, 2 * subgrid_len), backward, preferred_element...]
    reshape x0 -> x4, local copies, waits for them, and re-layouts: none -> 7.49 us  [the longest x2 4.02 us: on_device(): return (resid.reshape(observed.shape), image.reshape(facets.shape))]
    unnamed x41 -> x0, local copies, waits for them, and re-layouts: 4.9 us -> none
  transfers between devices with their start and end apart: 1 -> 0, of which waited for: 0 -> 0; matrix products, arithmetic and copies ran while one was open for 8% -> 0% of each run, Pallas kernels for 0% -> 0%
where the time goes in v1:
time: 59.8 us; the launch traced here: 59.3 us
  Pallas kernels  51.2 us (86%)
  local copies, waits for them, and re-layouts  7.49 us (13%)
  between operations  0.65 us (1%)
    pallas_call x1, Pallas kernels, join(): pl.pallas_call(functools.partial(join_kernel, work, pol, vis), out_shape=...  13.6 us
    pallas_call x1, Pallas kernels, visibilities(): pl.pallas_call(functools.partial(visibility_kernel, pols), out_shape=(jax...  10.9 us
    pallas_call x1, Pallas kernels, spread(): pl.pallas_call(functools.partial(spread_kernel, work, vis), out_shape=jax...  9.65 us
    pallas_call x1, Pallas kernels, backward(): pl.pallas_call(functools.partial(backward_kernel, facet_total, count, chu...  9.03 us
    pallas_call x1, Pallas kernels, forward(): pl.pallas_call(functools.partial(forward_kernel, facet_total, pols * line...  7.94 us
    reshape x2, local copies, waits for them, and re-layouts, on_device(): return (resid.reshape(observed.shape), image.reshape(facets.shape))  4.02 us
    reshape x1, local copies, waits for them, and re-layouts, forward(): facets.reshape(rows, width_two)  1.95 us
    reshape x1, local copies, waits for them, and re-layouts, on_device(): subs, seen = join(part, observed.reshape(blocks, 2 * pols, slots), sizes)  1.53 us

profile of v1, /device:TPU:0, one launch (start us, length us, event | category | flops | bytes accessed | tf_op | source)
XLA Modules:
  0.0 59.3 jit_solution(5008904667105884329)
XLA Ops:
  0.6 1.5 %reshape.24.obs_ref = f32[4,4,1024]{2,1,0:T(4,128)} reshape(f32[4,2,2,1024]{3,2,1,0:T(2,128)} %param.15) | data formatting | bytes 131072 | tf_op jit(solution)/shard_map/reshape | solution.py:493
  2.2 2.0 %reshape.22.fac_ref = bf16[128,2048]{1,0:T(8,128)(2,1)} reshape(bf16[16,2,4,2048]{3,2,1,0:T(4,128)(2,1)} %param.8) | data formatting | bytes 1048576 | tf_op jit(solution)/shard_map/reshape | solution.py:117
  4.1 7.9 %forward.1 = bf16[8,8,1024]{2,1,0:T(8,128)(2,1)} custom-call(s32[8]{0:T(128)} %off_ref.3, bf16[128,2048]{1,0:T(8,128)(2,1)} %reshape.22.fac_ref), custom_call_target="tpu_custom_call" | custom-call | tf_op jit(solution)/shard_map/forward/pallas_call | solution.py:103
  12.0 13.6 %join.1 = (bf16[2,2,2,8,1024]{4,3,2,1,0:T(8,128)(2,1)}, f32[2,4,4,1024]{3,2,1,0:T(4,128)}) custom-call(bf16[4,2,8,1024]{3,2,1,0:T(8,128)(2,1)} %bitcast.3, f32[4,4,1024]{2,1,0:T(4,128)} %reshape.24.obs_ref), custom_call_target="tpu_custom_call" | custom-call | tf_op jit(solution)/shard_map/join/pallas_call | solution.py:426
  25.7 10.9 %visibilities.1 = (f32[4,4,1024]{2,1,0:T(4,128)}, bf16[2,2,8,1024]{3,2,1,0:T(8,128)(2,1)}) custom-call(s32[4]{0:T(128)} %which_ref.1, s32[4]{0:T(128)} %count_ref.1, f32[4,2,1024]{2,1,0:T(2,128)} %coord_ref.1, s32[4,2,1024]{2,1,0:T(2,128)} %stat_ref.1, f32[8,512]{1,0:T(8,128)} %jones_ref.1, f32[2,4,4,1024]{3,2,1,0:T(4,128)} %get-tuple-element.6.obs_ref, ...), custom_call_target="tpu_custom_call" | custom-call | tf_op jit(solution)/shard_map/visibilities/pallas_call | solution.py:336
  36.6 1.5 %reshape.25 = f32[4,2,2,1024]{3,2,1,0:T(2,128)} reshape(f32[4,4,1024]{2,1,0:T(4,128)} %get-tuple-element.8) | data formatting | bytes 131072 | tf_op jit(solution)/shard_map/reshape | solution.py:503
  38.1 9.6 %spread.1 = bf16[4,2,8,1024]{3,2,1,0:T(8,128)(2,1)} custom-call(bf16[2,2,8,1024]{3,2,1,0:T(8,128)(2,1)} %get-tuple-element.9.part_ref), custom_call_target="tpu_custom_call" | custom-call | tf_op jit(solution)/shard_map/spread/pallas_call | solution.py:470
  47.8 9.0 %backward.1 = f32[128,2048]{1,0:T(8,128)} custom-call(s32[8]{0:T(128)} %off_ref.3, bf16[8,8,1024]{2,1,0:T(8,128)(2,1)} %bitcast.2), custom_call_target="tpu_custom_call" | custom-call | tf_op jit(solution)/shard_map/backward/pallas_call | solution.py:174
  56.8 2.5 %reshape.27 = f32[16,2,4,2048]{3,2,1,0:T(4,128)} reshape(f32[128,2048]{1,0:T(8,128)} %backward.1) | data formatting | bytes 2097152 | tf_op jit(solution)/shard_map/reshape | solution.py:503

commit v2 on v0

v2 whole, which is shorter than its diff:
```python
import functools
import math

import jax
import jax.numpy as jnp
from jax import lax
from jax.experimental import pallas as pl
from jax.experimental.pallas import tpu as pltpu
from jax.sharding import PartitionSpec as P

SS = 512
STEP = 32
MESH = pl.DeviceIdType.MESH
F32 = jnp.float32
BF16 = jnp.bfloat16
VMEM = pl.BlockSpec(memory_space=pltpu.VMEM)
ANY = pl.BlockSpec(memory_space=pl.ANY)
SMEM = pl.BlockSpec(memory_space=pltpu.SMEM)
LIMIT = 60 * 1024 * 1024


def sincos(turns):
    y = (turns - jnp.floor(turns + 0.5)) * (0.5 * math.pi)
    q = y * y
    s = y * (1.0 + q * (-1 / 6 + q * (1 / 120 + q * (-1 / 5040 + q * (1 / 362880)))))
    c = 1.0 + q * (-1 / 2 + q * (1 / 24 + q * (-1 / 720 + q * (1 / 40320))))
    for _ in range(2):
        s, c = 2.0 * s * c, 1.0 - 2.0 * s * s
    return s, c


def iota(shape, axis):
    return lax.broadcasted_iota(jnp.int32, shape, axis)


def int_turns(product, length):
    return lax.rem(product, length).astype(F32) * (1.0 / length)


def fill_table(cos_ref, sin_ref, image_len):
    rows, cols = cos_ref.shape
    coarse = rows // STEP
    sa, ca = sincos(-int_turns(iota((coarse, cols), 0) * STEP * iota((coarse, cols), 1), image_len))
    sb, cb = sincos(-int_turns(iota((STEP, cols), 0) * iota((STEP, cols), 1), image_len))
    for a in range(coarse):
        s, c = sa[a : a + 1], ca[a : a + 1]
        cos_ref[a * STEP : (a + 1) * STEP, :] = (c * cb - s * sb).astype(BF16)
        sin_ref[a * STEP : (a + 1) * STEP, :] = (s * cb + c * sb).astype(BF16)


def cmul(a, b):
    return (a[0] * b[0] - a[1] * b[1], a[0] * b[1] + a[1] * b[0])


def conj(a):
    return (a[0], -a[1])


def cadd(a, b):
    return (a[0] + b[0], a[1] + b[1])


def pick(flag, a, b):
    return (jnp.where(flag, a[0], b[0]), jnp.where(flag, a[1], b[1]))


def send(src, dst, send_sem, recv_sem, device):
    copy = pltpu.make_async_remote_copy(
        src_ref=src, dst_ref=dst, send_sem=send_sem, recv_sem=recv_sem,
        device_id=device, device_id_type=MESH,
    )
    copy.start()
    return copy


def ahead(name, size, hop):
    return lax.rem(lax.axis_index(name) + hop, size)


def dot(a, b):
    return jnp.dot(a, b, preferred_element_type=F32)


def kernel(
    sizes, off_ref, which_ref, count_ref, fac_hbm, coord_ref, stat_ref, jones_ref, obs_ref,
    resid_ref, image_ref,
    fac_ref, wide_ref, fcos_ref, fsin_ref, bcos_ref, bsin_ref, re_ref, im_ref, bre_ref, bim_ref,
    part_ref, land_ref, subs_ref, seen_ref, wave_ref, phase_ref, gain_ref, hot_ref, stack_ref,
    weight_ref, grid_ref, gpart_ref, gland_ref, grids_ref, image_acc,
    fac_sem, s_work, r_work, s_out, r_out, s_obs, r_obs, s_vis, r_vis, s_grid, r_grid,
):
    work, pol, vis = sizes
    count, pols, lines, width_two = fac_ref.shape
    cells = width_two // 2
    per_facet = pols * lines
    rows = count * per_facet
    subs = part_ref.shape[1]
    facet_total = count * work
    image_len = facet_total * cells
    blocks, _, slots = coord_ref.shape
    all_rows = lines * vis
    total = pols * pol
    me, my_pol, my_vis = (lax.axis_index(n) for n in ("work", "pol", "vis"))
    start = me * count

    def peer(d):
        return {"work": ahead("work", work, d)}

    mates = [
        {"pol": ahead("pol", pol, a), "vis": ahead("vis", vis, b)}
        for a in range(pol) for b in range(vis) if a + b > 0
    ]
    everyone = [peer(d) for d in range(1, work)] + mates
    fetch = pltpu.make_async_copy(fac_hbm, fac_ref, fac_sem)
    fetch.start()
    barrier = pltpu.get_barrier_semaphore()
    for device in everyone:
        pl.semaphore_signal(barrier, inc=1, device_id=device, device_id_type=MESH)
    fill_table(fcos_ref, fsin_ref, image_len)
    fetch.wait()
    for f in range(count):
        for p in range(pols):
            row = f * per_facet + p * lines
            wide_ref[row : row + lines, :] = fac_ref[f, p].astype(F32)
    pl.semaphore_wait(barrier, len(everyone))
    seen_copies = [
        send(obs_ref, seen_ref.at[my_pol], s_obs.at[a - 1], r_obs.at[a - 1],
             {"pol": ahead("pol", pol, a)})
        for a in range(1, pol)
    ]
    seen_ref[my_pol] = obs_ref[...]

    def share(d):
        slot = jnp.maximum(d - 1, 0) if isinstance(d, int) else d - 1
        return pltpu.make_async_remote_copy(
            src_ref=part_ref.at[ahead("work", work, d)], dst_ref=land_ref.at[slot],
            send_sem=s_work.at[slot], recv_sem=r_work.at[slot],
            device_id=peer(d), device_id_type=MESH,
        )

    def forward_step(d):
        owner = ahead("work", work, d)
        for i in range(subs):
            offset = off_ref[owner * subs + i]
            s, c = sincos(-int_turns(iota((1, cells), 1) * offset, image_len))
            real, imag = wide_ref[:, :cells], wide_ref[:, cells:]
            re_ref[i * rows : (i + 1) * rows, :] = (real * c - imag * s).astype(BF16)
            im_ref[i * rows : (i + 1) * rows, :] = (real * s + imag * c).astype(BF16)
        real_spec = dot(re_ref[...], fcos_ref[...]) - dot(im_ref[...], fsin_ref[...])
        imag_spec = dot(re_ref[...], fsin_ref[...]) + dot(im_ref[...], fcos_ref[...])
        scale = 1.0 / math.sqrt(image_len)
        for i in range(subs):
            offset = off_ref[owner * subs + i]
            ids = start + iota((count, SS), 0)
            s, c = sincos(-int_turns(ids * (offset + iota((count, SS), 1)), facet_total))
            real = imag = 0.0
            for f in range(count):
                first = i * rows + f * per_facet
                a = real_spec[first : first + per_facet]
                b = imag_spec[first : first + per_facet]
                real += a * c[f : f + 1] - b * s[f : f + 1]
                imag += a * s[f : f + 1] + b * c[f : f + 1]
            part_ref[owner, i, :, :SS] = (real * scale).astype(BF16)
            part_ref[owner, i, :, SS:] = (imag * scale).astype(BF16)

    def forward_loop(d, carry):
        forward_step(d)

        @pl.when(d < work)
        def _():
            share(d).start()

        return carry

    lax.fori_loop(1, work + 1, forward_loop, 0)

    own_subs = subs_ref.at[my_pol, my_vis]
    spread = [
        pltpu.make_async_remote_copy(
            src_ref=own_subs, dst_ref=own_subs, send_sem=s_out.at[i], recv_sem=r_out.at[i],
            device_id=mate, device_id_type=MESH,
        )
        for i, mate in enumerate(mates)
    ]

    def gather_shares():
        def add(d, carry):
            share(d).wait()
            stack_ref[:, :per_facet, :] += land_ref[d - 1].astype(F32)
            return carry

        stack_ref[:, :per_facet, :] = part_ref[me].astype(F32)
        lax.fori_loop(1, work, add, 0)
        subs_ref[my_pol, my_vis] = stack_ref[:, :per_facet, :].astype(BF16)
        for copy in spread:
            copy.start()

    table = jones_ref[...]
    high = table.astype(BF16)
    rest = table - high.astype(F32)
    middle = rest.astype(BF16)
    low_part = (rest - middle.astype(F32)).astype(BF16)
    parts = jnp.concatenate([high, middle, low_part], 0)
    entries = table.shape[0]
    coarse = SS // STEP

    def prepare(t, carry):
        @pl.when(t == blocks // 2)
        def _():
            gather_shares()

        m, l = coord_ref[t, 1:2, :], coord_ref[t, 0:1, :]
        sa, ca = sincos(iota((coarse, slots), 0).astype(F32) * STEP * m)
        sb, cb = sincos(iota((STEP, slots), 0).astype(F32) * m)
        for a in range(coarse):
            s, c = sa[a : a + 1], ca[a : a + 1]
            wave_ref[t, a * STEP : (a + 1) * STEP, :] = (c * cb - s * sb).astype(BF16)
            wave_ref[t, SS + a * STEP : SS + (a + 1) * STEP, :] = (s * cb + c * sb).astype(BF16)
        sr, cr = sincos(iota((all_rows, slots), 0).astype(F32) * l)
        phase_ref[t, 0] = cr
        phase_ref[t, 1] = sr
        for side in range(2):
            hot = iota((table.shape[1], slots), 0) == stat_ref[t, side : side + 1, :]
            hot_ref[...] = jnp.where(hot, 1.0, 0.0).astype(BF16)
            got = dot(parts, hot_ref[...])
            got = (got[2 * entries :] + got[entries : 2 * entries]) + got[:entries]
            gain_ref[t, side] = got
        return carry

    lax.fori_loop(0, blocks, prepare, 0)

    for copy in seen_copies + spread:
        copy.wait()
    for g in range(subs):
        for p in range(total):
            for h in range(vis):
                at = (p % pols) * lines
                both = subs_ref[p // pols, h, g, at : at + lines, :].astype(F32)
                real, imag = both[:, :SS], both[:, SS:]
                row = p * all_rows + h * lines
                low = total * all_rows + row
                stack_ref[g, row : row + lines, :SS] = real
                stack_ref[g, row : row + lines, SS:] = -imag
                stack_ref[g, low : low + lines, :SS] = imag
                stack_ref[g, low : low + lines, SS:] = real
    grid_ref[...] = jnp.zeros_like(grid_ref)
    scale = 1.0 / math.sqrt(all_rows * SS)
    mine = my_pol * pols

    def degrid(t, carry):
        which = which_ref[t]
        cr, sr = phase_ref[t, 0], phase_ref[t, 1]
        chosen = stack_ref[0]
        for g in range(1, subs):
            chosen = jnp.where(which == g, stack_ref[g], chosen)
        product = dot(chosen.astype(BF16), wave_ref[t])
        model = []
        for p in range(total):
            low = (total + p) * all_rows
            y_re = product[p * all_rows : (p + 1) * all_rows]
            y_im = product[low : low + all_rows]
            re = jnp.sum(cr * y_re - sr * y_im, axis=0, keepdims=True) * scale
            im = jnp.sum(cr * y_im + sr * y_re, axis=0, keepdims=True) * scale
            model.append((re, im))
        half = entries // 2
        left, right = (
            [[(gain_ref[t, side, 2 * i + k : 2 * i + k + 1, :],
               gain_ref[t, side, half + 2 * i + k : half + 2 * i + k + 1, :])
              for k in range(2)] for i in range(2)]
            for side in range(2)
        )
        bright = [[model[2 * i + k] for k in range(2)] for i in range(2)]
        inner = [[cadd(cmul(left[i][0], bright[0][k]), cmul(left[i][1], bright[1][k]))
                  for k in range(2)] for i in range(2)]
        outer = [[cadd(cmul(inner[i][0], conj(right[k][0])), cmul(inner[i][1], conj(right[k][1])))
                  for k in range(2)] for i in range(2)]
        live = iota((1, slots), 1) < count_ref[t]
        resid = []
        for p in range(total):
            got = outer[p // 2][p % 2]
            resid.append(tuple(
                jnp.where(live, seen_ref[p // pols, t, p % pols, n : n + 1, :] - got[n], 0.0)
                for n in range(2)
            ))
        for j in range(pols):
            p = mine + j
            own = resid[0]
            for other in range(1, total):
                own = pick(p == other, resid[other], own)
            resid_ref[t, j, 0:1, :] = own[0]
            resid_ref[t, j, 1:2, :] = own[1]
            first, second = p < 2, lax.rem(p, 2) == 0
            l0 = conj(pick(first, left[0][0], left[0][1]))
            l1 = conj(pick(first, left[1][0], left[1][1]))
            r0 = pick(second, right[0][0], right[0][1])
            r1 = pick(second, right[1][0], right[1][1])
            t0 = cadd(cmul(l0, resid[0]), cmul(l1, resid[2]))
            t1 = cadd(cmul(l0, resid[1]), cmul(l1, resid[3]))
            cre, cim = cadd(cmul(t0, r0), cmul(t1, r1))
            row = 2 * j * all_rows
            weight_ref[row : row + all_rows, :] = cr * cre + sr * cim
            weight_ref[row + all_rows : row + 2 * all_rows, :] = cr * cim - sr * cre
        summed = lax.dot_general(
            weight_ref[...].astype(BF16), wave_ref[t], (((1,), (1,)), ((), ())),
            preferred_element_type=F32,
        )
        for g in range(subs):
            grid_ref[g] += jnp.where(which == g, summed, 0.0)
        return carry

    lax.fori_loop(0, blocks, degrid, 0)

    for g in range(subs):
        for j in range(pols):
            row = 2 * j * all_rows
            real_z = grid_ref[g, row : row + all_rows, :]
            imag_z = grid_ref[g, row + all_rows : row + 2 * all_rows, :]
            real = ((real_z[:, :SS] + imag_z[:, SS:]) * scale).astype(BF16)
            imag = ((imag_z[:, :SS] - real_z[:, SS:]) * scale).astype(BF16)
            for h in range(vis):
                cut = slice(h * lines, (h + 1) * lines)
                gpart_ref[h, g, j * lines : (j + 1) * lines, :SS] = real[cut]
                gpart_ref[h, g, j * lines : (j + 1) * lines, SS:] = imag[cut]
    halves = [
        send(gpart_ref.at[ahead("vis", vis, b)], gland_ref.at[b - 1], s_vis.at[b - 1],
             r_vis.at[b - 1], {"vis": ahead("vis", vis, b)})
        for b in range(1, vis)
    ]
    fill_table(bcos_ref, bsin_ref, image_len)
    both = gpart_ref[my_vis].astype(F32)
    for b, copy in enumerate(halves):
        copy.wait()
        both += gland_ref[b].astype(F32)
    grids_ref[me] = both.astype(BF16)

    def grid_copy(d):
        own = grids_ref.at[me]
        return pltpu.make_async_remote_copy(
            src_ref=own, dst_ref=own, send_sem=s_grid.at[d - 1], recv_sem=r_grid.at[d - 1],
            device_id=peer(d), device_id_type=MESH,
        )

    for d in range(1, work):
        grid_copy(d).start()
    image_acc[...] = jnp.zeros_like(image_acc)

    def backward_step(d, carry):
        @pl.when(d > 0)
        def _():
            grid_copy(d).wait()

        owner = ahead("work", work, work - d)
        for i in range(subs):
            offset = off_ref[owner * subs + i]
            ids = start + iota((count, SS), 0)
            s, c = sincos(int_turns(ids * (offset + iota((count, SS), 1)), facet_total))
            real = grids_ref[owner, i, :, :SS].astype(F32)
            imag = grids_ref[owner, i, :, SS:].astype(F32)
            for f in range(count):
                first = i * rows + f * per_facet
                sf, cf = s[f : f + 1], c[f : f + 1]
                bre_ref[first : first + per_facet, :] = (real * cf - imag * sf).astype(BF16)
                bim_ref[first : first + per_facet, :] = (real * sf + imag * cf).astype(BF16)
        real_img = dot(bre_ref[...], bcos_ref[...]) + dot(bim_ref[...], bsin_ref[...])
        imag_img = dot(bim_ref[...], bcos_ref[...]) - dot(bre_ref[...], bsin_ref[...])
        unit = 1.0 / math.sqrt(image_len)
        real_sum = imag_sum = 0.0
        for i in range(subs):
            offset = off_ref[owner * subs + i]
            s, c = sincos(int_turns(iota((1, cells), 1) * offset, image_len))
            s, c = s * unit, c * unit
            a = real_img[i * rows : (i + 1) * rows]
            b = imag_img[i * rows : (i + 1) * rows]
            real_sum += a * c - b * s
            imag_sum += a * s + b * c
        image_acc[:, :cells] += real_sum
        image_acc[:, cells:] += imag_sum
        return carry

    lax.fori_loop(0, work, backward_step, 0)
    for f in range(count):
        for p in range(pols):
            row = f * per_facet + p * lines
            image_ref[f, p] = image_acc[row : row + lines, :]


def on_device(
    sizes, facets, subgrid_offset, tile_subgrid, tile_count, vis_coord, stations, jones, observed
):
    work, pol, vis = sizes
    count, pols, lines, width_two = facets.shape
    blocks, _, _, slots = observed.shape
    subs = subgrid_offset.shape[0] // work
    cells, wide = width_two // 2, pols * lines
    rows = count * wide
    all_rows, total = lines * vis, pols * pol
    block = (subs, wide, 2 * SS)
    dma = pltpu.SemaphoreType.DMA
    mates = pol * vis - 1
    return pl.pallas_call(
        functools.partial(kernel, sizes),
        out_shape=(
            jax.ShapeDtypeStruct(observed.shape, F32),
            jax.ShapeDtypeStruct(facets.shape, F32),
        ),
        in_specs=[SMEM, SMEM, SMEM, ANY, VMEM, VMEM, VMEM, VMEM],
        out_specs=(VMEM, VMEM),
        scratch_shapes=[
            pltpu.VMEM(facets.shape, BF16),
            pltpu.VMEM((rows, width_two), F32),
            pltpu.VMEM((cells, SS), BF16),
            pltpu.VMEM((cells, SS), BF16),
            pltpu.VMEM((SS, cells), BF16),
            pltpu.VMEM((SS, cells), BF16),
            pltpu.VMEM((subs * rows, cells), BF16),
            pltpu.VMEM((subs * rows, cells), BF16),
            pltpu.VMEM((subs * rows, SS), BF16),
            pltpu.VMEM((subs * rows, SS), BF16),
            pltpu.VMEM((work,) + block, BF16),
            pltpu.VMEM((work - 1,) + block, BF16),
            pltpu.VMEM((pol, vis) + block, BF16),
            pltpu.VMEM((pol,) + observed.shape, F32),
            pltpu.VMEM((blocks, 2 * SS, slots), BF16),
            pltpu.VMEM((blocks, 2, all_rows, slots), F32),
            pltpu.VMEM((blocks, 2) + (jones.shape[0], slots), F32),
            pltpu.VMEM((jones.shape[1], slots), BF16),
            pltpu.VMEM((subs, 2 * total * all_rows, 2 * SS), F32),
            pltpu.VMEM((2 * pols * all_rows, slots), F32),
            pltpu.VMEM((subs, 2 * pols * all_rows, 2 * SS), F32),
            pltpu.VMEM((vis,) + block, BF16),
            pltpu.VMEM((vis - 1,) + block, BF16),
            pltpu.VMEM((work,) + block, BF16),
            pltpu.VMEM((rows, width_two), F32),
            dma,
            dma((work - 1,)), dma((work - 1,)), dma((mates,)), dma((mates,)),
            dma((pol - 1,)), dma((pol - 1,)), dma((vis - 1,)), dma((vis - 1,)),
            dma((work - 1,)), dma((work - 1,)),
        ],
        compiler_params=pltpu.CompilerParams(
            collective_id=0, has_side_effects=True, vmem_limit_bytes=LIMIT
        ),
        name="cycle",
    )(subgrid_offset, tile_subgrid, tile_count, facets, vis_coord, stations, jones, observed)


def solution(mesh):
    sizes = tuple(mesh.shape[name] for name in ("work", "pol", "vis"))
    in_specs = (
        P(("groups", "work"), "pol", "vis", None),
        P("groups"),
        P(("groups", "work", "vis")),
        P(("groups", "work", "vis")),
        P(("groups", "work", "vis"), None, None),
        P(("work", "vis"), None, None),
        P(None, "groups"),
        P(("groups", "work", "vis"), "pol", None, None),
    )
    out_specs = (
        P(("groups", "work", "vis"), "pol", None, None),
        P(("groups", "work"), "pol", "vis", None),
    )
    return jax.shard_map(
        functools.partial(on_device, sizes),
        mesh=mesh, in_specs=in_specs, out_specs=out_specs, check_vma=False,
    )
```

time: 220 us -> 38.6 us (0.18)
  other arithmetic: 111 us -> 0 us
  blocking collectives: 50.6 us -> 0 us
  Pallas kernels: 0 us -> 33.9 us
  local copies, waits for them, and re-layouts: 28.9 us -> 3.78 us
  between operations: 16 us -> 0.64 us
  matrix products: 13.4 us -> 0 us
    another operation x19 -> x0, other arithmetic: 99.2 us -> none
    pallas_call x0 -> x1, Pallas kernels: none -> 33.9 us  [on_device(): pl.pallas_call(functools.partial(kernel, sizes), out_shape=(jax.ShapeDtyp...]
    unnamed x1 -> x0, blocking collectives: 25.8 us -> none
    all_gather x4 -> x0, blocking collectives: 24.8 us -> none  [the longest x1 13.6 us: on_device(): lax.all_gather(grid_half, 'work', axis=0, tiled=True)]
    gather x4 -> x0, local copies, waits for them, and re-layouts: 22.7 us -> none  [jones_matrix(): picked = jnp.take(table, pairs[:, column, :], axis=1)]
    dot_general x4 -> x0, matrix products: 13.4 us -> none  [the longest x1 4.53 us: to_facets(): jnp.dot(rotated.reshape(-1, 2 * subgrid_len), backward, preferred_element...]
    cos x3 -> x0, other arithmetic: 3.63 us -> none  [the longest x1 2.77 us: to_facets(): cosine_in = jnp.cos(turn_in)[:, :, None, None, :]]
    convert_element_type x12 -> x0, other arithmetic: 3.23 us -> none  [the longest x1 0.93 us: on_device(): residual_vis.astype(jnp.bfloat16)]
  transfers between devices with their start and end apart: 1 -> 0, of which waited for: 0 -> 0; matrix products, arithmetic and copies ran while one was open for 8% -> 0% of each run, Pallas kernels for 0% -> 0%
where the time goes in v2:
time: 38.6 us; the launch traced here: 38.3 us
  Pallas kernels  33.9 us (88%)
  local copies, waits for them, and re-layouts  3.78 us (10%)
  between operations  0.64 us (2%)
    pallas_call x1, Pallas kernels, on_device(): pl.pallas_call(functools.partial(kernel, sizes), out_shape=(jax.ShapeDtyp...  33.9 us
    unnamed x2, local copies, waits for them, and re-layouts  3.78 us

profile of v2, /device:TPU:0, one launch (start us, length us, event | category | flops | bytes accessed | tf_op | source)
XLA Modules:
  0.0 38.3 jit_solution(5790767948454237762)
XLA Ops:
  0.6 33.9 %cycle.1 = (f32[4,2,2,1024]{3,2,1,0:T(2,128)}, f32[16,2,4,2048]{3,2,1,0:T(4,128)}) custom-call(s32[8]{0:T(128)} %off_ref.1, s32[4]{0:T(128)} %which_ref.1, s32[4]{0:T(128)} %count_ref.1, bf16[16,2,4,2048]{3,2,1,0:T(4,128)(2,1)} %fac_hbm.1, f32[4,2,1024]{2,1,0:T(2,128)} %coord_ref.1, s32[4,2,1024]{2,1,0:T(2,128)} %stat_ref.1, f32[8,512]{1,0:T(8,128)} %jones_ref.1, ...), custom_call_target="tpu_custom_call" | custom-call | tf_op jit(solution)/shard_map/cycle/pallas_call | solution.py:400
  34.5 1.5 %copy.12 = f32[4,2,2,1024]{3,2,1,0:T(2,128)} copy(f32[4,2,2,1024]{3,2,1,0:T(2,128)} %get-tuple-element.4) | data formatting | bytes 131072
  36.0 2.3 %copy.13 = f32[16,2,4,2048]{3,2,1,0:T(4,128)} copy(f32[16,2,4,2048]{3,2,1,0:T(4,128)} %get-tuple-element.5) | data formatting | bytes 2097152

commit v3 on v2

--- a/solution.py
+++ b/solution.py
@@ -14,9 +14,8 @@
 F32 = jnp.float32
 BF16 = jnp.bfloat16
 VMEM = pl.BlockSpec(memory_space=pltpu.VMEM)
-ANY = pl.BlockSpec(memory_space=pl.ANY)
 SMEM = pl.BlockSpec(memory_space=pltpu.SMEM)
-LIMIT = 60 * 1024 * 1024
+LIMIT = 30 * 1024 * 1024
 
 
 def sincos(turns):
@@ -82,12 +81,12 @@
 
 
 def kernel(
-    sizes, off_ref, which_ref, count_ref, fac_hbm, coord_ref, stat_ref, jones_ref, obs_ref,
+    sizes, off_ref, which_ref, count_ref, fac_ref, coord_ref, stat_ref, jones_ref, obs_ref,
     resid_ref, image_ref,
-    fac_ref, wide_ref, fcos_ref, fsin_ref, bcos_ref, bsin_ref, re_ref, im_ref, bre_ref, bim_ref,
+    wide_ref, fcos_ref, fsin_ref, bcos_ref, bsin_ref, re_ref, im_ref, bre_ref, bim_ref,
     part_ref, land_ref, subs_ref, seen_ref, wave_ref, phase_ref, gain_ref, hot_ref, stack_ref,
     weight_ref, grid_ref, gpart_ref, gland_ref, grids_ref, image_acc,
-    fac_sem, s_work, r_work, s_out, r_out, s_obs, r_obs, s_vis, r_vis, s_grid, r_grid,
+    s_work, r_work, s_out, r_out, s_obs, r_obs, s_vis, r_vis, s_grid, r_grid,
 ):
     work, pol, vis = sizes
     count, pols, lines, width_two = fac_ref.shape
@@ -111,13 +110,10 @@
         for a in range(pol) for b in range(vis) if a + b > 0
     ]
     everyone = [peer(d) for d in range(1, work)] + mates
-    fetch = pltpu.make_async_copy(fac_hbm, fac_ref, fac_sem)
-    fetch.start()
     barrier = pltpu.get_barrier_semaphore()
     for device in everyone:
         pl.semaphore_signal(barrier, inc=1, device_id=device, device_id_type=MESH)
     fill_table(fcos_ref, fsin_ref, image_len)
-    fetch.wait()
     for f in range(count):
         for p in range(pols):
             row = f * per_facet + p * lines
@@ -210,18 +206,22 @@
             gather_shares()
 
         m, l = coord_ref[t, 1:2, :], coord_ref[t, 0:1, :]
-        sa, ca = sincos(iota((coarse, slots), 0).astype(F32) * STEP * m)
-        sb, cb = sincos(iota((STEP, slots), 0).astype(F32) * m)
+        sa, ca = (x.astype(BF16) for x in sincos(iota((coarse, slots), 0).astype(F32) * STEP * m))
+        sb, cb = (x.astype(BF16) for x in sincos(iota((STEP, slots), 0).astype(F32) * m))
         for a in range(coarse):
             s, c = sa[a : a + 1], ca[a : a + 1]
-            wave_ref[t, a * STEP : (a + 1) * STEP, :] = (c * cb - s * sb).astype(BF16)
-            wave_ref[t, SS + a * STEP : SS + (a + 1) * STEP, :] = (s * cb + c * sb).astype(BF16)
+            wave_ref[t, a * STEP : (a + 1) * STEP, :] = c * cb - s * sb
+            wave_ref[t, SS + a * STEP : SS + (a + 1) * STEP, :] = s * cb + c * sb
         sr, cr = sincos(iota((all_rows, slots), 0).astype(F32) * l)
         phase_ref[t, 0] = cr
         phase_ref[t, 1] = sr
         for side in range(2):
-            hot = iota((table.shape[1], slots), 0) == stat_ref[t, side : side + 1, :]
-            hot_ref[...] = jnp.where(hot, 1.0, 0.0).astype(BF16)
+            station = stat_ref[t, side : side + 1, :]
+            near = jnp.where(iota((STEP, slots), 0) == station % STEP, 1.0, 0.0).astype(BF16)
+            groups = table.shape[1] // STEP
+            far = jnp.where(iota((groups, slots), 0) == station // STEP, 1.0, 0.0).astype(BF16)
+            for a in range(groups):
+                hot_ref[a * STEP : (a + 1) * STEP, :] = far[a : a + 1] * near
             got = dot(parts, hot_ref[...])
             got = (got[2 * entries :] + got[entries : 2 * entries]) + got[:entries]
             gain_ref[t, side] = got
@@ -403,10 +403,9 @@
             jax.ShapeDtypeStruct(observed.shape, F32),
             jax.ShapeDtypeStruct(facets.shape, F32),
         ),
-        in_specs=[SMEM, SMEM, SMEM, ANY, VMEM, VMEM, VMEM, VMEM],
+        in_specs=[SMEM, SMEM, SMEM, VMEM, VMEM, VMEM, VMEM, VMEM],
         out_specs=(VMEM, VMEM),
         scratch_shapes=[
-            pltpu.VMEM(facets.shape, BF16),
             pltpu.VMEM((rows, width_two), F32),
             pltpu.VMEM((cells, SS), BF16),
             pltpu.VMEM((cells, SS), BF16),
@@ -431,7 +430,6 @@
             pltpu.VMEM((vis - 1,) + block, BF16),
             pltpu.VMEM((work,) + block, BF16),
             pltpu.VMEM((rows, width_two), F32),
-            dma,
             dma((work - 1,)), dma((work - 1,)), dma((mates,)), dma((mates,)),
             dma((pol - 1,)), dma((pol - 1,)), dma((vis - 1,)), dma((vis - 1,)),
             dma((work - 1,)), dma((work - 1,)),

time: 38.6 us -> 41.1 us (1.065)
  local copies, waits for them, and re-layouts: 3.78 us -> 7.67 us
  Pallas kernels: 33.9 us -> 32.4 us
    unnamed x2 -> x18, local copies, waits for them, and re-layouts: 3.78 us -> 7.67 us
    pallas_call x1, Pallas kernels: 33.9 us -> 32.4 us  [on_device(): pl.pallas_call(functools.partial(kernel, sizes), out_shape=(jax.ShapeDtyp...]
where the time goes in v3:
time: 41.1 us; the launch traced here: 40.7 us
  Pallas kernels  32.4 us (79%)
  local copies, waits for them, and re-layouts  7.67 us (19%)
  between operations  0.66 us (2%)
    pallas_call x1, Pallas kernels, on_device(): pl.pallas_call(functools.partial(kernel, sizes), out_shape=(jax.ShapeDtyp...  32.4 us
    unnamed x18, local copies, waits for them, and re-layouts  7.67 us

profile of v3, /device:TPU:0, one launch (start us, length us, event | category | flops | bytes accessed | tf_op | source)
XLA Modules:
  0.0 40.7 jit_solution(9253781990579861774)
XLA Ops:
  0.6 0.0 copy-start
  0.6 1.0 %copy-done = bf16[16,2,4,2048]{3,2,1,0:T(4,128)(2,1)S(1)} copy-done((bf16[16,2,4,2048]{3,2,1,0:T(4,128)(2,1)S(1)}, bf16[16,2,4,2048]{3,2,1,0:T(4,128)(2,1)}, u32[]{:S(2)}) %copy-start) | copy-done | bytes 524312
  1.7 0.0 copy-start.1
  1.7 0.8 %copy-done.1 = f32[4,2,2,1024]{3,2,1,0:T(2,128)S(1)} copy-done((f32[4,2,2,1024]{3,2,1,0:T(2,128)S(1)}, f32[4,2,2,1024]{3,2,1,0:T(2,128)}, u32[]{:S(2)}) %copy-start.1) | copy-done | bytes 65560
  2.5 0.0 copy-start.2
  2.5 0.8 %copy-done.2 = f32[4,2,1024]{2,1,0:T(2,128)S(1)} copy-done((f32[4,2,1024]{2,1,0:T(2,128)S(1)}, f32[4,2,1024]{2,1,0:T(2,128)}, u32[]{:S(2)}) %copy-start.2) | copy-done | bytes 32792
  3.3 0.0 copy-start.3
  3.3 0.8 %copy-done.3 = s32[4,2,1024]{2,1,0:T(2,128)S(1)} copy-done((s32[4,2,1024]{2,1,0:T(2,128)S(1)}, s32[4,2,1024]{2,1,0:T(2,128)}, u32[]{:S(2)}) %copy-start.3) | copy-done | bytes 32792
  4.0 0.0 copy-start.4
  4.0 0.7 %copy-done.4 = f32[8,512]{1,0:T(8,128)S(1)} copy-done((f32[8,512]{1,0:T(8,128)S(1)}, f32[8,512]{1,0:T(8,128)}, u32[]{:S(2)}) %copy-start.4) | copy-done | bytes 16408
  4.8 0.0 copy-start.5
  4.8 0.7 %copy-done.5 = s32[8]{0:T(128)S(1)} copy-done((s32[8]{0:T(128)S(1)}, s32[8]{0:T(128)}, u32[]{:S(2)}) %copy-start.5) | copy-done | bytes 56
  5.4 0.0 copy-start.6
  5.4 0.7 %copy-done.6 = s32[4]{0:T(128)S(1)} copy-done((s32[4]{0:T(128)S(1)}, s32[4]{0:T(128)}, u32[]{:S(2)}) %copy-start.6) | copy-done | bytes 40
  6.1 0.0 copy-start.7
  6.1 0.7 %copy-done.7 = s32[4]{0:T(128)S(1)} copy-done((s32[4]{0:T(128)S(1)}, s32[4]{0:T(128)}, u32[]{:S(2)}) %copy-start.7) | copy-done | bytes 40
  6.7 32.4 %cycle.1 = (f32[4,2,2,1024]{3,2,1,0:T(2,128)S(1)}, f32[16,2,4,2048]{3,2,1,0:T(4,128)S(1)}) custom-call(s32[8]{0:T(128)S(1)} %copy-done.5, s32[4]{0:T(128)S(1)} %copy-done.6, s32[4]{0:T(128)S(1)} %copy-done.7, bf16[16,2,4,2048]{3,2,1,0:T(4,128)(2,1)S(1)} %copy-done, f32[4,2,1024]{2,1,0:T(2,128)S(1)} %copy-done.2, s32[4,2,1024]{2,1,0:T(2,128)S(1)} %copy-done.3, ...), custom_call_target="tpu_custom_call" | custom-call | tf_op jit(solution)/shard_map/cycle/pallas_call | solution.py:400
  39.1 0.6 %copy.12 = f32[4,2,2,1024]{3,2,1,0:T(2,128)} copy(f32[4,2,2,1024]{3,2,1,0:T(2,128)S(1)} %get-tuple-element.4) | data formatting | bytes 131072
  39.7 1.0 %copy.13 = f32[16,2,4,2048]{3,2,1,0:T(4,128)} copy(f32[16,2,4,2048]{3,2,1,0:T(4,128)S(1)} %get-tuple-element.5) | data formatting | bytes 2097152
Async XLA Ops:
  0.6 1.0 %copy-start = (bf16[16,2,4,2048]{3,2,1,0:T(4,128)(2,1)S(1)}, bf16[16,2,4,2048]{3,2,1,0:T(4,128)(2,1)}, u32[]{:S(2)}) copy-start(bf16[16,2,4,2048]{3,2,1,0:T(4,128)(2,1)} %fac_ref.1) | copy-start | bytes 1572868
  1.7 0.8 %copy-start.1 = (f32[4,2,2,1024]{3,2,1,0:T(2,128)S(1)}, f32[4,2,2,1024]{3,2,1,0:T(2,128)}, u32[]{:S(2)}) copy-start(f32[4,2,2,1024]{3,2,1,0:T(2,128)} %obs_ref.1) | copy-start | bytes 196612
  2.5 0.8 %copy-start.2 = (f32[4,2,1024]{2,1,0:T(2,128)S(1)}, f32[4,2,1024]{2,1,0:T(2,128)}, u32[]{:S(2)}) copy-start(f32[4,2,1024]{2,1,0:T(2,128)} %coord_ref.1) | copy-start | bytes 98308
  3.3 0.8 %copy-start.3 = (s32[4,2,1024]{2,1,0:T(2,128)S(1)}, s32[4,2,1024]{2,1,0:T(2,128)}, u32[]{:S(2)}) copy-start(s32[4,2,1024]{2,1,0:T(2,128)} %stat_ref.1) | copy-start | bytes 98308
  4.0 0.7 %copy-start.4 = (f32[8,512]{1,0:T(8,128)S(1)}, f32[8,512]{1,0:T(8,128)}, u32[]{:S(2)}) copy-start(f32[8,512]{1,0:T(8,128)} %jones_ref.1) | copy-start | bytes 49156
  4.8 0.7 %copy-start.5 = (s32[8]{0:T(128)S(1)}, s32[8]{0:T(128)}, u32[]{:S(2)}) copy-start(s32[8]{0:T(128)} %off_ref.1) | copy-start | bytes 100
  5.4 0.7 %copy-start.6 = (s32[4]{0:T(128)S(1)}, s32[4]{0:T(128)}, u32[]{:S(2)}) copy-start(s32[4]{0:T(128)} %which_ref.1) | copy-start | bytes 52
  6.1 0.7 %copy-start.7 = (s32[4]{0:T(128)S(1)}, s32[4]{0:T(128)}, u32[]{:S(2)}) copy-start(s32[4]{0:T(128)} %count_ref.1) | copy-start | bytes 52

commit v4 on v3

--- a/solution.py
+++ b/solution.py
@@ -14,6 +14,7 @@
 F32 = jnp.float32
 BF16 = jnp.bfloat16
 VMEM = pl.BlockSpec(memory_space=pltpu.VMEM)
+HBM = pl.BlockSpec(memory_space=pltpu.HBM)
 SMEM = pl.BlockSpec(memory_space=pltpu.SMEM)
 LIMIT = 30 * 1024 * 1024
 
@@ -81,12 +82,12 @@
 
 
 def kernel(
-    sizes, off_ref, which_ref, count_ref, fac_ref, coord_ref, stat_ref, jones_ref, obs_ref,
+    sizes, off_ref, which_ref, count_ref, fac_hbm, coord_ref, stat_ref, jones_ref, obs_ref,
     resid_ref, image_ref,
-    wide_ref, fcos_ref, fsin_ref, bcos_ref, bsin_ref, re_ref, im_ref, bre_ref, bim_ref,
+    fac_ref, wide_ref, fcos_ref, fsin_ref, bcos_ref, bsin_ref, re_ref, im_ref, bre_ref, bim_ref,
     part_ref, land_ref, subs_ref, seen_ref, wave_ref, phase_ref, gain_ref, hot_ref, stack_ref,
     weight_ref, grid_ref, gpart_ref, gland_ref, grids_ref, image_acc,
-    s_work, r_work, s_out, r_out, s_obs, r_obs, s_vis, r_vis, s_grid, r_grid,
+    fac_sem, s_work, r_work, s_out, r_out, s_obs, r_obs, s_vis, r_vis, s_grid, r_grid,
 ):
     work, pol, vis = sizes
     count, pols, lines, width_two = fac_ref.shape
@@ -110,10 +111,13 @@
         for a in range(pol) for b in range(vis) if a + b > 0
     ]
     everyone = [peer(d) for d in range(1, work)] + mates
+    fetch = pltpu.make_async_copy(fac_hbm, fac_ref, fac_sem)
+    fetch.start()
     barrier = pltpu.get_barrier_semaphore()
     for device in everyone:
         pl.semaphore_signal(barrier, inc=1, device_id=device, device_id_type=MESH)
     fill_table(fcos_ref, fsin_ref, image_len)
+    fetch.wait()
     for f in range(count):
         for p in range(pols):
             row = f * per_facet + p * lines
@@ -403,9 +407,10 @@
             jax.ShapeDtypeStruct(observed.shape, F32),
             jax.ShapeDtypeStruct(facets.shape, F32),
         ),
-        in_specs=[SMEM, SMEM, SMEM, VMEM, VMEM, VMEM, VMEM, VMEM],
+        in_specs=[SMEM, SMEM, SMEM, HBM, VMEM, VMEM, VMEM, VMEM],
         out_specs=(VMEM, VMEM),
         scratch_shapes=[
+            pltpu.VMEM(facets.shape, BF16),
             pltpu.VMEM((rows, width_two), F32),
             pltpu.VMEM((cells, SS), BF16),
             pltpu.VMEM((cells, SS), BF16),
@@ -430,6 +435,7 @@
             pltpu.VMEM((vis - 1,) + block, BF16),
             pltpu.VMEM((work,) + block, BF16),
             pltpu.VMEM((rows, width_two), F32),
+            dma,
             dma((work - 1,)), dma((work - 1,)), dma((mates,)), dma((mates,)),
             dma((pol - 1,)), dma((pol - 1,)), dma((vis - 1,)), dma((vis - 1,)),
             dma((work - 1,)), dma((work - 1,)),
@@ -438,7 +444,11 @@
             collective_id=0, has_side_effects=True, vmem_limit_bytes=LIMIT
         ),
         name="cycle",
-    )(subgrid_offset, tile_subgrid, tile_count, facets, vis_coord, stations, jones, observed)
+    )(*(
+        pltpu.with_memory_space_constraint(x, pltpu.HBM)
+        for x in (subgrid_offset, tile_subgrid, tile_count, facets, vis_coord, stations, jones,
+                  observed)
+    ))
 
 
 def solution(mesh):

time: 41.1 us -> 35.2 us (0.86)
  local copies, waits for them, and re-layouts: 7.67 us -> 1.6 us
    unnamed x18 -> x2, local copies, waits for them, and re-layouts: 7.67 us -> 1.6 us
where the time goes in v4:
time: 35.2 us; the launch traced here: 35 us
  Pallas kernels  32.8 us (93%)
  local copies, waits for them, and re-layouts  1.6 us (5%)
  between operations  0.64 us (2%)
    pallas_call x1, Pallas kernels, on_device(): pl.pallas_call(functools.partial(kernel, sizes), out_shape=(jax.ShapeDtyp...  32.8 us
    unnamed x2, local copies, waits for them, and re-layouts  1.6 us

profile of v4, /device:TPU:0, one launch (start us, length us, event | category | flops | bytes accessed | tf_op | source)
XLA Modules:
  0.0 35.0 jit_solution(14024255071298620521)
XLA Ops:
  0.6 32.8 %cycle.1 = (f32[4,2,2,1024]{3,2,1,0:T(2,128)S(1)}, f32[16,2,4,2048]{3,2,1,0:T(4,128)S(1)}) custom-call(s32[8]{0:T(128)} %off_ref.1, s32[4]{0:T(128)} %which_ref.1, s32[4]{0:T(128)} %count_ref.1, bf16[16,2,4,2048]{3,2,1,0:T(4,128)(2,1)} %fac_hbm.1, f32[4,2,1024]{2,1,0:T(2,128)} %coord_ref.1, s32[4,2,1024]{2,1,0:T(2,128)} %stat_ref.1, f32[8,512]{1,0:T(8,128)} %jones_ref.1, ...), custom_call_target="tpu_custom_call" | custom-call | tf_op jit(solution)/shard_map/cycle/pallas_call | solution.py:404
  33.4 0.6 %copy.12 = f32[4,2,2,1024]{3,2,1,0:T(2,128)} copy(f32[4,2,2,1024]{3,2,1,0:T(2,128)S(1)} %get-tuple-element.4) | data formatting | bytes 131072
  34.0 1.0 %copy.13 = f32[16,2,4,2048]{3,2,1,0:T(4,128)} copy(f32[16,2,4,2048]{3,2,1,0:T(4,128)S(1)} %get-tuple-element.5) | data formatting | bytes 2097152
